TPU v7x, 128 devices: a whole 4x4x4 slice. The times are simulated.
128 devices in a mesh: kv: 32 (over y, z, x_hi), pb: 4 (over x_lo, core).
Axes of the slice: x: 4 (x_hi: 2, x_lo: 2; x = x_hi * 2 + x_lo), y: 4, z: 4, core: 2. Of those that a mesh axis runs over, the one named last changes fastest.
Arguments:
- queries: bfloat16 [49152, 4096], P('kv', 'pb'), may hold values from -12 to 12
- cached_keys: bfloat16 [32, 256, 4096], P('kv', None, 'pb'), may hold values from -6 to 6
- cached_values: bfloat16 [32, 256, 4096], P('kv', None, 'pb'), may hold values from -6 to 6
- block_map: int32 [768, 1], P('kv'), may hold values from 0 to 31; in each aligned block of 24 rows (0 to 23, 24 to 47, ...) at most 2 rows name the same one
- out_weight: bfloat16 [4096, 4096], P('pb'), may hold values from -0.09375 to 0.09375
- hidden: bfloat16 [49152, 4096], P('kv', 'pb'), may hold values from -6 to 6
Outputs:
- mixed: bfloat16 [49152, 4096], P('kv', 'pb')
Inputs may be any that keep to these rules, and one draw needn't show every extreme that they name: `block_map`: at most 2 of the 24 spans of one index of kv name the same block, and some index has a block named by exactly 2 of its spans; every block is named by some span.
All inputs are finite; a program needn't handle non-finite values.
Results may differ from a plain program's by a relative error of at most 0.0085.
Values may be sent and summed in bfloat16 or wider, within the bound.
No kernel may reach another device: no remote copies, remote signals or barrier semaphores. Data moves between devices by JAX's collectives and lax.ppermute only.
A program may use at most 192 MiB of HBM per device.

v0:
```python
import jax
import jax.numpy as jnp
from jax import lax
from jax.sharding import PartitionSpec as P

HEAD = 128
SPAN = 64


def attend(span_queries, keys_now, values_now):
    item_count, row_count, feat_width = span_queries.shape
    key_count = keys_now.shape[0]
    head_count = feat_width // HEAD
    query_heads = span_queries.reshape(item_count, row_count, head_count, HEAD)
    key_heads = keys_now.reshape(key_count, head_count, HEAD)
    value_heads = values_now.reshape(key_count, head_count, HEAD)
    scores = jnp.einsum(
        "nrhd,khd->nhrk", query_heads, key_heads, preferred_element_type=jnp.float32
    ) * HEAD ** (-0.5)
    row_top = jnp.max(scores, axis=-1, keepdims=True)
    exponent = jnp.exp(scores - row_top)
    weights = (exponent / jnp.sum(exponent, axis=-1, keepdims=True)).astype(jnp.bfloat16)
    result = jnp.einsum("nhrk,khd->nrhd", weights, value_heads, preferred_element_type=jnp.float32)
    return result.reshape(item_count, row_count, feat_width).astype(jnp.bfloat16)


def on_device(queries, cached_keys, cached_values, block_map, out_weight, hidden):
    tok_rows, feat_width = queries.shape
    span_count = tok_rows // SPAN
    q_spans = queries.reshape(span_count, SPAN, feat_width)
    block_count = lax.axis_size("kv")
    cap_slots = max(2, span_count // block_count)
    targets = block_map[:, 0]
    onehot = (targets[:, None] == jnp.arange(block_count, dtype=jnp.int32)[None, :]).astype(
        jnp.int32
    )
    earlier = jnp.cumsum(onehot, axis=0) - onehot
    position_in = jnp.sum(earlier * onehot, axis=1)
    slot_index = targets * cap_slots + position_in
    start_sum = jnp.zeros((span_count, SPAN, feat_width), jnp.float32)
    key_piece = lax.all_gather(cached_keys, "kv", axis=0, tiled=True)
    value_piece = lax.all_gather(cached_values, "kv", axis=0, tiled=True)

    def one_block(block_step, so_far):
        keys_now = lax.dynamic_index_in_dim(key_piece, block_step, 0, keepdims=False)
        values_now = lax.dynamic_index_in_dim(value_piece, block_step, 0, keepdims=False)
        wanted = block_step * cap_slots + jnp.arange(cap_slots, dtype=jnp.int32)
        picks = (slot_index[None, :] == wanted[:, None]).astype(jnp.bfloat16)
        chosen = jnp.einsum(
            "sc,crd->srd", picks, q_spans, preferred_element_type=jnp.float32
        ).astype(jnp.bfloat16)
        answer = attend(chosen, keys_now, values_now)
        return so_far + jnp.einsum("sc,srd->crd", picks, answer, preferred_element_type=jnp.float32)

    gathered_sum = lax.fori_loop(0, key_piece.shape[0], one_block, start_sum)
    attended = gathered_sum.astype(jnp.bfloat16)
    flat_rows = attended.reshape(tok_rows, feat_width)
    partial_value = jnp.dot(flat_rows, out_weight, preferred_element_type=jnp.float32)
    summed = lax.psum_scatter(
        partial_value.astype(jnp.bfloat16), "pb", scatter_dimension=1, tiled=True
    ).astype(jnp.float32)
    return (hidden.astype(jnp.float32) + summed).astype(jnp.bfloat16)


def solution(mesh):
    placed = (
        P("kv", "pb"),
        P("kv", None, "pb"),
        P("kv", None, "pb"),
        P("kv", None),
        P("pb", None),
        P("kv", "pb"),
    )
    return jax.shard_map(
        on_device, mesh=mesh, in_specs=placed, out_specs=P("kv", "pb"), check_vma=False
    )
```

profile of v0, /device:TPU:1, one launch (start us, length us, event | category | flops | bytes accessed | tf_op | source)
XLA Modules:
  0.0 1246.2 jit_solution(3254958065707537142)
XLA Ops:
  12.7 156.4 %all-gather.5.cloned.1.call-done = bf16[32,256,1024]{2,1,0:T(8,128)(2,1)} async-done(((bf16[1,256,1024]{2,1,0:T(8,128)(2,1)}), bf16[32,256,1024]{2,1,0:T(8,128)(2,1)}) %all-gather.5.cloned.1.call-update) | async-done | bytes 16777232 | tf_op jit(solution)/shard_map/all_gather | solution.py:41
  169.1 157.2 %all-gather.3.cloned.1.call-done = bf16[32,256,1024]{2,1,0:T(8,128)(2,1)} async-done(((bf16[1,256,1024]{2,1,0:T(8,128)(2,1)}), bf16[32,256,1024]{2,1,0:T(8,128)(2,1)}) %all-gather.3.cloned.1.call-update) | async-done | bytes 16777232 | tf_op jit(solution)/shard_map/all_gather | solution.py:42
  326.2 774.2 %while.14 = (s32[]{:T(128)}, f32[24,64,1024]{2,0,1:T(8,128)}, s32[24]{0:T(128)S(1)}, bf16[32,256,1024]{2,1,0:T(8,128)(2,1)}, bf16[32,256,1024]{2,1,0:T(8,128)(2,...) while((s32[]{:T(128)}, f32[24,64,1024]{2,0,1:T(8,128)}, ...), condition=%wide.region_5.6_spmd.clone, body=%wide.region_2.5_spmd.clone.sunk | while | flops 152045168 | bytes 31465844 | solution.py:55
  366.2 6.6 select_add_fusion.2
  390.5 6.6 select_add_fusion.2
  414.7 6.6 select_add_fusion.2
  439.0 6.6 select_add_fusion.2
  463.2 6.6 select_add_fusion.2
  487.5 6.6 select_add_fusion.2
  536.0 6.6 select_add_fusion.2
  560.2 6.6 select_add_fusion.2
  584.5 6.6 select_add_fusion.2
  608.8 6.6 select_add_fusion.2
  633.0 6.6 select_add_fusion.2
  657.3 6.6 select_add_fusion.2
  681.5 6.6 select_add_fusion.2
  730.0 6.6 select_add_fusion.2
  754.3 6.6 select_add_fusion.2
  778.6 6.6 select_add_fusion.2
  802.8 6.6 select_add_fusion.2
  827.1 6.6 select_add_fusion.2
  851.3 6.6 select_add_fusion.2
  875.6 6.6 select_add_fusion.2
  899.8 6.6 select_add_fusion.2
  924.1 6.6 select_add_fusion.2
  972.6 6.6 select_add_fusion.2
  996.9 6.6 select_add_fusion.2
  1021.1 6.6 select_add_fusion.2
  1069.6 6.6 select_add_fusion.2
  1093.9 6.6 select_add_fusion.2
  1106.8 15.7 %convolution_convert_fusion.2 = bf16[1536,4096]{1,0:T(8,128)(2,1)} fusion(bf16[1536,1024]{1,0:T(8,128)(2,1)S(1)} %bitcast.78, bf16[1024,4096]{1,0:T(8,128)(2,1)S(1)} %copy-done.3), kind=kOutput, calls=%fused_computation.27 | convolution fusion | flops 12891193344 | bytes 24117248 | tf_op jit(solution)/shard_map/dot_general | solution.py:58
  1122.5 112.0 %reduce-scatter.2.cloned.1.call-done = bf16[1536,1024]{1,0:T(8,128)(2,1)} async-done(((bf16[1536,4096]{1,0:T(8,128)(2,1)}), bf16[1536,1024]{1,0:T(8,128)(2,1)}) %reduce-scatter.2.cloned.1.call-update) | async-done | bytes 3145744 | tf_op jit(solution)/shard_map/reduce_scatter | solution.py:59
  (473 shorter events, 612.8 us)
Async XLA Ops:
  6.5 5.9 copy-start.2
  6.5 162.5 %all-gather.5.cloned.1.call-start = ((), (), s32[]{:S(2)}) async-start(), calls=%async_computation.2 | async-start | bytes 17301504 | tf_op jit(solution)/shard_map/all_gather | solution.py:41
  7.3 319.0 %all-gather.3.cloned.1.call-start = ((), (), s32[]{:S(2)}) async-start(), calls=%async_computation.1 | async-start | bytes 17301504 | tf_op jit(solution)/shard_map/all_gather | solution.py:42
  8.0 1226.5 %reduce-scatter.2.cloned.1.call-start = ((), (), s32[]{:S(2)}) async-start(), calls=%async_computation.3 | async-start | bytes 15728640 | tf_op jit(solution)/shard_map/reduce_scatter | solution.py:59
  336.6 1.0 copy-start
  359.0 1.0 copy-start
  383.2 1.0 copy-start
  407.5 1.0 copy-start
  431.7 1.0 copy-start
  456.0 1.0 copy-start
  480.2 1.0 copy-start
  504.5 1.0 copy-start
  528.7 1.0 copy-start
  553.0 1.0 copy-start
  577.3 1.0 copy-start
  601.5 1.0 copy-start
  625.8 1.0 copy-start
  650.0 1.0 copy-start
  674.3 1.0 copy-start
  698.5 1.0 copy-start
  722.8 1.0 copy-start
  747.1 1.0 copy-start
  771.3 1.0 copy-start
  819.8 1.0 copy-start
  844.1 1.0 copy-start
  868.3 1.0 copy-start
  892.6 1.0 copy-start
  916.8 1.0 copy-start
  965.3 1.0 copy-start
  1038.1 1.0 copy-start
  1100.5 6.3 copy-start.3
  1122.5 112.1 %copy-start.1 = (bf16[1536,1024]{1,0:T(8,128)(2,1)S(1)}, bf16[1536,1024]{1,0:T(8,128)(2,1)}, u32[]{:S(2)}) copy-start(bf16[1536,1024]{1,0:T(8,128)(2,1)} %param.13) | copy-start | bytes 9437188
  (6 other events, 5.8 us)
Sparse Core Ops, SparseCore 0:
  10.4 158.6 all-gather.4
  172.1 154.0 all-gather.2
  1122.6 111.8 reduce-scatter.1
where the time goes:
time: 1260 us; the launch traced here: 1250 us
  waiting for transfers between devices  427 us (34%)
  matrix products  420 us (33%)
  local copies, waits for them, and re-layouts  366 us (29%)
  other arithmetic  18.7 us (1%)
  between operations  13.1 us (1%)
    dot_general x32, matrix products, one_block(): jnp.einsum('sc,srd->crd', picks, answer, preferred_element_type=jnp.float32)  209 us
    all_gather x1, waiting for transfers between devices, on_device(): value_piece = lax.all_gather(cached_values, 'kv', axis=0, tiled=True)  157 us
    all_gather x1, waiting for transfers between devices, on_device(): key_piece = lax.all_gather(cached_keys, 'kv', axis=0, tiled=True)  156 us
    dynamic_slice x64, local copies, waits for them, and re-layouts, one_block(): lax.dynamic_index_in_dim(key_piece, block_step, 0, keepdims=False)  139 us
    dot_general x32, matrix products, attend(): jnp.einsum('nhrk,khd->nrhd', weights, value_heads, preferred_element_type...  128 us
    reduce_scatter x1, waiting for transfers between devices, on_device(): lax.psum_scatter(partial_value.astype(jnp.bfloat16), 'pb', scatter_dimens...  112 us
    dynamic_slice x32, local copies, waits for them, and re-layouts, one_block(): lax.dynamic_index_in_dim(value_piece, block_step, 0, keepdims=False)  66.1 us
    reshape x64, local copies, waits for them, and re-layouts, attend(): query_heads = span_queries.reshape(item_count, row_count, head_count, HEAD)  60.5 us
  transfers between devices with their start and end apart: 3, of which 3 were waited for; matrix products, arithmetic and copies ran while one was open for 0% of the time, Pallas kernels for 0%

commit v1 on v0

v1 whole, which is shorter than its diff:
```python
import functools

import jax
import jax.numpy as jnp
from jax import lax
from jax.experimental import pallas as pl
from jax.experimental.pallas import tpu as pltpu
from jax.sharding import PartitionSpec as P

HEAD = 128
SPAN = 64
LOG2E = 1.4426950408889634


def attend_kernel(map_ref, q_ref, k_ref, v_ref, o_ref):
    head_count = q_ref.shape[-1] // HEAD
    scale = LOG2E * HEAD ** (-0.5)
    for head in range(head_count):
        cols = slice(head * HEAD, (head + 1) * HEAD)
        scores = lax.dot_general(
            q_ref[:, cols],
            k_ref[0, :, cols],
            (((1,), (1,)), ((), ())),
            preferred_element_type=jnp.float32,
        )
        row_top = jnp.max(scores, axis=-1, keepdims=True)
        exponent = jnp.exp2((scores - row_top) * scale)
        total = jnp.sum(exponent, axis=-1, keepdims=True)
        result = jnp.dot(
            exponent.astype(jnp.bfloat16), v_ref[0, :, cols], preferred_element_type=jnp.float32
        )
        o_ref[:, cols] = (result / total).astype(jnp.bfloat16)


def attend(queries, keys, values, targets):
    tok_rows, feat_width = queries.shape
    key_count = keys.shape[1]
    span_count = tok_rows // SPAN
    return pl.pallas_call(
        attend_kernel,
        out_shape=jax.ShapeDtypeStruct((tok_rows, feat_width), jnp.bfloat16),
        grid_spec=pltpu.PrefetchScalarGridSpec(
            num_scalar_prefetch=1,
            grid=(span_count,),
            in_specs=[
                pl.BlockSpec((SPAN, feat_width), lambda i, m: (i, 0)),
                pl.BlockSpec((1, key_count, feat_width), lambda i, m: (m[i], 0, 0)),
                pl.BlockSpec((1, key_count, feat_width), lambda i, m: (m[i], 0, 0)),
            ],
            out_specs=pl.BlockSpec((SPAN, feat_width), lambda i, m: (i, 0)),
        ),
        name="attend",
    )(targets, queries, keys, values)


def on_device(queries, cached_keys, cached_values, block_map, out_weight, hidden):
    targets = block_map[:, 0]
    key_piece = lax.all_gather(cached_keys, "kv", axis=0, tiled=True)
    value_piece = lax.all_gather(cached_values, "kv", axis=0, tiled=True)
    attended = attend(queries, key_piece, value_piece, targets)
    partial_value = jnp.dot(attended, out_weight, preferred_element_type=jnp.float32)
    summed = lax.psum_scatter(
        partial_value.astype(jnp.bfloat16), "pb", scatter_dimension=1, tiled=True
    ).astype(jnp.float32)
    return (hidden.astype(jnp.float32) + summed).astype(jnp.bfloat16)


def solution(mesh):
    placed = (
        P("kv", "pb"),
        P("kv", None, "pb"),
        P("kv", None, "pb"),
        P("kv", None),
        P("pb", None),
        P("kv", "pb"),
    )
    return jax.shard_map(
        on_device, mesh=mesh, in_specs=placed, out_specs=P("kv", "pb"), check_vma=False
    )
```

time: 1260 us -> 522 us (0.41); the launches traced: 1250 us -> 522 us
  matrix products: 420 us -> 19.8 us
  local copies, waits for them, and re-layouts: 366 us -> 0.01 us
  Pallas kernels: 0 us -> 52.4 us
  other arithmetic: 18.7 us -> 5.08 us
    dot_general x97 -> x1, matrix products: 378 us -> 19.8 us  [on_device(): jnp.dot(attended, out_weight, preferred_element_type=jnp.float32)]
    dynamic_slice x96 -> x0, local copies, waits for them, and re-layouts: 205 us -> none  [the longest x64 139 us: one_block(): lax.dynamic_index_in_dim(key_piece, block_step, 0, keepdims=False)]
    reshape x64 -> x0, local copies, waits for them, and re-layouts: 60.5 us -> none  [attend(): query_heads = span_queries.reshape(item_count, row_count, head_count, HEAD)]
    convert_element_type x64 -> x0, local copies, waits for them, and re-layouts: 60.5 us -> none  [attend(): result.reshape(item_count, row_count, feat_width).astype(jnp.bfloat16)]
    pallas_call x0 -> x1, Pallas kernels: none -> 52.4 us  [attend(): pl.pallas_call(attend_kernel, out_shape=jax.ShapeDtypeStruct((tok_rows, f...]
    while x32 -> x0, matrix products: 42.2 us -> none
    while x65 -> x0, local copies, waits for them, and re-layouts: 37.1 us -> none
where the time goes in v1:
time: 522 us
  waiting for transfers between devices  432 us (83%)
  Pallas kernels  52.4 us (10%)
  matrix products  19.8 us (4%)
  between operations  13.1 us (3%)
    all_gather x1, waiting for transfers between devices, on_device(): key_piece = lax.all_gather(cached_keys, 'kv', axis=0, tiled=True)  161 us
    all_gather x1, waiting for transfers between devices, on_device(): value_piece = lax.all_gather(cached_values, 'kv', axis=0, tiled=True)  157 us
    reduce_scatter x1, waiting for transfers between devices, on_device(): lax.psum_scatter(partial_value.astype(jnp.bfloat16), 'pb', scatter_dimens...  112 us
    pallas_call x1, Pallas kernels, attend(): pl.pallas_call(attend_kernel, out_shape=jax.ShapeDtypeStruct((tok_rows, f...  52.4 us
    dot_general x1, matrix products, on_device(): jnp.dot(attended, out_weight, preferred_element_type=jnp.float32)  19.8 us
  transfers between devices with their start and end apart: 3, of which 3 were waited for; matrix products, arithmetic and copies ran while one was open for 0% of the time, Pallas kernels for 0%

profile of v1, /device:TPU:1, one launch (start us, length us, event | category | flops | bytes accessed | tf_op | source)
XLA Modules:
  0.0 522.1 jit_solution(14214083618182587365)
XLA Ops:
  6.5 0.0 all-gather.3.cloned.1.call-start
  6.5 0.7 all-gather.3.cloned.1.call-update
  7.3 0.0 all-gather.5.cloned.1.call-start
  7.3 0.7 all-gather.5.cloned.1.call-update
  8.0 0.0 reduce-scatter.2.cloned.1.call-start
  8.1 161.0 %all-gather.3.cloned.1.call-done.k_ref = bf16[32,256,1024]{2,1,0:T(8,128)(2,1)} async-done(((bf16[1,256,1024]{2,1,0:T(8,128)(2,1)}), bf16[32,256,1024]{2,1,0:T(8,128)(2,1)}) %all-gather.3.cloned.1.call-update) | async-done | bytes 16777232 | tf_op jit(solution)/shard_map/all_gather | solution.py:58
  169.1 157.2 %all-gather.5.cloned.1.call-done.v_ref = bf16[32,256,1024]{2,1,0:T(8,128)(2,1)} async-done(((bf16[1,256,1024]{2,1,0:T(8,128)(2,1)}), bf16[32,256,1024]{2,1,0:T(8,128)(2,1)}) %all-gather.5.cloned.1.call-update) | async-done | bytes 16777232 | tf_op jit(solution)/shard_map/all_gather | solution.py:59
  326.2 52.4 %attend.1 = bf16[1536,1024]{1,0:T(8,128)(2,1)} custom-call(s32[24]{0:T(128)} %bitcast.3, bf16[1536,1024]{1,0:T(8,128)(2,1)} %q_ref.1, bf16[32,256,1024]{2,1,0:T(8,128)(2,1)} %all-gather.3.cloned.1.call-done.k_ref, bf16[32,256,1024]{2,1,0:T(8,128)(2,1)} %all-gather.5.cloned.1.call-done.v_ref), custom_call_target="tpu_custom_call" | custom-call | tf_op jit(solution)/shard_map/attend/pallas_call | solution.py:39
  378.6 19.8 %convolution_convert_fusion = bf16[1536,4096]{1,0:T(8,128)(2,1)} fusion(bf16[1536,1024]{1,0:T(8,128)(2,1)} %attend.1, bf16[1024,4096]{1,0:T(8,128)(2,1)} %param.10), kind=kOutput, calls=%fused_computation | convolution fusion | flops 12891193344 | bytes 24117248 | tf_op jit(solution)/shard_map/dot_general | solution.py:61
  398.4 0.0 copy-start
  398.4 0.0 reduce-scatter.2.cloned.1.call-update
  398.5 112.0 %reduce-scatter.2.cloned.1.call-done = bf16[1536,1024]{1,0:T(8,128)(2,1)} async-done(((bf16[1536,4096]{1,0:T(8,128)(2,1)}), bf16[1536,1024]{1,0:T(8,128)(2,1)}) %reduce-scatter.2.cloned.1.call-update) | async-done | bytes 3145744 | tf_op jit(solution)/shard_map/reduce_scatter | solution.py:62
  510.5 0.0 copy-done
  510.5 5.1 add_convert_fusion
Async XLA Ops:
  6.5 162.5 %all-gather.3.cloned.1.call-start = ((), (), s32[]{:S(2)}) async-start(), calls=%async_computation.1 | async-start | bytes 17301504 | tf_op jit(solution)/shard_map/all_gather | solution.py:58
  7.3 319.0 %all-gather.5.cloned.1.call-start = ((), (), s32[]{:S(2)}) async-start(), calls=%async_computation.2 | async-start | bytes 17301504 | tf_op jit(solution)/shard_map/all_gather | solution.py:59
  8.0 502.5 %reduce-scatter.2.cloned.1.call-start = ((), (), s32[]{:S(2)}) async-start(), calls=%async_computation.3 | async-start | bytes 15728640 | tf_op jit(solution)/shard_map/reduce_scatter | solution.py:62
  398.4 112.1 %copy-start = (bf16[1536,1024]{1,0:T(8,128)(2,1)S(1)}, bf16[1536,1024]{1,0:T(8,128)(2,1)}, u32[]{:S(2)}) copy-start(bf16[1536,1024]{1,0:T(8,128)(2,1)} %param.11) | copy-start | bytes 9437188
Sparse Core Ops, SparseCore 0:
  10.4 158.6 all-gather.2
  172.1 154.0 all-gather.4
  398.6 111.8 reduce-scatter.1

commit v2 on v1

v2 whole, which is shorter than its diff:
```python
import functools

import jax
import jax.numpy as jnp
from jax import lax
from jax.experimental import pallas as pl
from jax.experimental.pallas import tpu as pltpu
from jax.sharding import PartitionSpec as P


HEAD = 128
SPAN = 64
LOG2E = 1.4426950408889634
PLANES = [[i * 2 + half for i in range(16)] for half in range(2)]
SIDE = 4
JOINT_A, RING_A, RING_B, JOINT_B = (0, 1), (2, 3), (4, 5), (6, 7)


def pb_flip(bits):
    return [(i, i ^ bits) for i in range(4)]


def far_flip(bits):
    return [(kv * 4 + pb, (kv ^ 1) * 4 + (pb ^ bits)) for kv in range(32) for pb in range(4)]


def kv_index(y, z, half):
    return ((y % SIDE) * SIDE + z % SIDE) * 2 + half


def kv_shift(dy, dz):
    return [
        (kv_index(y, z, half), kv_index(y + dy, z + dz, half))
        for y in range(SIDE)
        for z in range(SIDE)
        for half in range(2)
    ]


def attend_kernel(first_col, part_count, spot_ref, q_hbm, *refs):
    key_parts, value_parts = refs[:part_count], refs[part_count : 2 * part_count]
    o_ref, q_buf, k_buf, v_buf, sems, q_sem = refs[2 * part_count :]
    tok_rows, width = o_ref.shape
    span_count = tok_rows // SPAN
    head_count = width // HEAD
    scale = LOG2E * HEAD ** (-0.5)
    at_once = max(1, 8 // head_count)
    while span_count % at_once:
        at_once -= 1

    q_copy = pltpu.make_async_copy(q_hbm.at[:, pl.ds(first_col, width)], q_buf, q_sem)
    q_copy.start()

    def fetch(parts, held, side, span):
        for i, part in enumerate(parts):

            @pl.when(spot_ref[2 * side, span] == i)
            def _():
                pltpu.make_async_copy(
                    part.at[spot_ref[2 * side + 1, span]], held.at[span], sems.at[side, span]
                ).start()

    def start_span(span, carry):
        fetch(key_parts, k_buf, 0, span)
        fetch(value_parts, v_buf, 1, span)
        return carry

    lax.fori_loop(0, span_count, start_span, 0)
    q_copy.wait()

    def some_spans(step, carry):
        units = []
        for near in range(at_once):
            span = step * at_once + near
            pltpu.make_async_copy(key_parts[0].at[0], k_buf.at[span], sems.at[0, span]).wait()
            pltpu.make_async_copy(value_parts[0].at[0], v_buf.at[span], sems.at[1, span]).wait()
            rows = pl.ds(pl.multiple_of(span * SPAN, SPAN), SPAN)
            for head in range(head_count):
                units.append((span, rows, slice(head * HEAD, (head + 1) * HEAD)))
        scores = [
            lax.dot_general(
                q_buf[rows, cols],
                k_buf[span, :, cols],
                (((1,), (1,)), ((), ())),
                preferred_element_type=jnp.float32,
            )
            for span, rows, cols in units
        ]
        tops = [jnp.max(part, axis=-1, keepdims=True) for part in scores]
        exponents = [jnp.exp2((part - top) * scale) for part, top in zip(scores, tops)]
        totals = [jnp.sum(part, axis=-1, keepdims=True) for part in exponents]
        results = [
            jnp.dot(
                part.astype(jnp.bfloat16),
                v_buf[span, :, cols],
                preferred_element_type=jnp.float32,
            )
            for part, (span, rows, cols) in zip(exponents, units)
        ]
        for result, total, (span, rows, cols) in zip(results, totals, units):
            o_ref[rows, cols] = (result / total).astype(jnp.bfloat16)
        return carry

    lax.fori_loop(0, span_count // at_once, some_spans, 0)


def attend(spots, queries, first_col, key_parts, value_parts):
    tok_rows = queries.shape[0]
    span_count = tok_rows // SPAN
    key_count, width = key_parts[0].shape[1:]
    flops = 4 * tok_rows * key_count * width
    held = pltpu.VMEM((span_count, key_count, width), jnp.bfloat16)
    return pl.pallas_call(
        functools.partial(attend_kernel, first_col, len(key_parts)),
        out_shape=jax.ShapeDtypeStruct((tok_rows, width), jnp.bfloat16),
        grid_spec=pltpu.PrefetchScalarGridSpec(
            num_scalar_prefetch=1,
            grid=(1,),
            in_specs=[pl.BlockSpec(memory_space=pl.ANY)] * (1 + 2 * len(key_parts)),
            out_specs=pl.BlockSpec((tok_rows, width), lambda i, s: (0, 0)),
            scratch_shapes=[
                pltpu.VMEM((tok_rows, width), jnp.bfloat16),
                held,
                held,
                pltpu.SemaphoreType.DMA((2, span_count)),
                pltpu.SemaphoreType.DMA,
            ],
        ),
        compiler_params=pltpu.CompilerParams(vmem_limit_bytes=60 << 20),
        cost_estimate=pl.CostEstimate(
            flops=flops, bytes_accessed=20 << 20, transcendentals=0
        ),
        name="attend",
    )(spots, queries, *key_parts, *value_parts)


def project_kernel(base_ref, *refs):
    count = len(refs) // 2
    total = base_ref[...].astype(jnp.float32)
    for i in range(count):
        total += jnp.dot(refs[i][...], refs[count + i][...], preferred_element_type=jnp.float32)
    refs[-1][...] = total.astype(refs[-1].dtype)


def project(base, pairs, out_type):
    tok_rows, out_width = base.shape
    rows = tok_rows // 6
    features = [part for part, _, _ in pairs]
    weights = [part for _, part, _ in pairs]
    wide = pl.BlockSpec((rows, out_width), lambda i: (i, 0))

    def held(width, place):
        return pl.BlockSpec((width, out_width), lambda i: (place, 0))

    depth = sum(part.shape[1] for part in features)
    return pl.pallas_call(
        project_kernel,
        out_shape=jax.ShapeDtypeStruct((tok_rows, out_width), out_type),
        grid=(6,),
        in_specs=[wide]
        + [pl.BlockSpec((rows, part.shape[1]), lambda i: (i, 0)) for part in features]
        + [held(part.shape[1], place) for part, _, place in pairs],
        out_specs=wide,
        compiler_params=pltpu.CompilerParams(vmem_limit_bytes=40 << 20),
        cost_estimate=pl.CostEstimate(
            flops=2 * tok_rows * depth * out_width, bytes_accessed=20 << 20, transcendentals=0
        ),
    )(base, *features, *weights)


def near_ring(block, plus, minus):
    up = lax.ppermute(block, "kv", minus)
    down = lax.ppermute(block, "kv", plus)
    far = lax.ppermute(block, "kv", twice(minus))
    return jnp.concatenate([block, up, far, down])


def twice(steps):
    following = dict(steps)
    return [(source, following[target]) for source, target in steps]


def both_ways(line, plus, minus):
    return lax.ppermute(line, "kv", minus), lax.ppermute(line, "kv", plus)


def pass_on(up, down, plus, minus):
    half = up.shape[0] // 2
    first = lax.ppermute(up[:half], "kv", minus)
    second = lax.ppermute(down[half:], "kv", plus)
    return first, second


def plane_gather(payload):
    return lax.all_gather(payload, "kv", axis=0, tiled=True, axis_index_groups=PLANES)


def exchange_weights(columns, pb, mid):
    core = lax.ppermute(columns(pb ^ 1), "pb", pb_flip(1))
    send2, send3 = columns(pb ^ 2), columns(pb ^ 3)
    near = [
        lax.ppermute(send2[:mid], "pb", pb_flip(2)),
        lax.ppermute(send2[mid:], ("kv", "pb"), far_flip(2)),
    ]
    cross = [
        lax.ppermute(send3[:mid], "pb", pb_flip(3)),
        lax.ppermute(send3[mid:], ("kv", "pb"), far_flip(3)),
    ]
    return core, near, cross


def on_device(queries, cached_keys, cached_values, block_map, out_weight, hidden):
    feat_width = queries.shape[1]
    me = lax.axis_index("kv")
    pb = lax.axis_index("pb")
    targets = block_map[:, 0]
    place, is_other = targets // 2, (targets + me) % 2
    step_y = (targets // 8 - me // 8) % SIDE
    step_z = (targets // 2 - me // 2) % SIDE
    joint_spot = place * 4 + is_other * 2
    whole = jnp.zeros_like(targets)
    joint_spots = jnp.stack([whole, joint_spot, whole, joint_spot + 1])

    def ring_part(far_step, near_step):
        flat = far_step * 8 + near_step * 2 + is_other
        part = jnp.where(far_step < 2, far_step, jnp.where(far_step == 3, 4, 2 + near_step // 2))
        return part, jnp.where(far_step == 2, flat % 4, flat % 8)

    ring_spots = jnp.stack([*ring_part(step_y, step_z), *ring_part(step_z, step_y)])
    swap = [(i, i ^ 1) for i in range(32)]
    y_plus, y_minus = kv_shift(1, 0), kv_shift(-1, 0)
    z_plus, z_minus = kv_shift(0, 1), kv_shift(0, -1)

    def cols_of(heads):
        return slice(heads[0] * HEAD, (heads[-1] + 1) * HEAD)

    own_both = jnp.concatenate([cached_keys, cached_values])

    def swapped(heads):
        own = own_both[:, :, cols_of(heads)]
        return jnp.concatenate([own, lax.ppermute(own, "kv", swap)])

    both_a = swapped(JOINT_A)
    ring_heads = RING_A + RING_B
    both_r = swapped(ring_heads)
    both_late = swapped(JOINT_B)
    y_ways, z_ways = (y_plus, y_minus), (z_plus, z_minus)
    key_line = near_ring(both_r[0::2], *z_ways)
    value_line = near_ring(both_r[1::2], *y_ways)
    out_weight, key_line, value_line = lax.optimization_barrier((out_weight, key_line, value_line))

    def columns(q):
        return lax.dynamic_slice_in_dim(out_weight, q * feat_width, feat_width, 1)

    mid = feat_width // 2
    weight_mine = columns(pb)
    weight_core, weight_near, weight_cross = exchange_weights(columns, pb, mid)

    def gather_heads(heads, mine):
        width = mine.shape[1]
        place, half_place = heads[0] * HEAD // width, heads[0] * HEAD % mid // width
        half = heads[0] * HEAD // mid
        core = lax.ppermute(mine, "pb", pb_flip(1))
        near = lax.ppermute(mine, "pb", pb_flip(2))
        cross = lax.ppermute(near, "pb", pb_flip(1))
        return [
            (mine, weight_mine, place),
            (core, weight_core, place),
            (near, weight_near[half], half_place),
            (cross, weight_cross[half], half_place),
        ]

    def by_joint(payload, heads):
        joint = plane_gather(payload)
        return attend(joint_spots, queries, heads[0] * HEAD, [joint], [joint])

    def sides(heads):
        first = heads[0] * HEAD - ring_heads[0] * HEAD
        cols = slice(first, first + len(heads) * HEAD)
        keys, values = key_line[:, :, cols], value_line[:, :, cols]
        return keys, both_ways(keys, *y_ways), values, both_ways(values, *z_ways)

    def by_ring(parts, heads):
        keys, key_sides, values, value_sides = parts
        key_far = pass_on(*key_sides, *y_ways)
        value_far = pass_on(*value_sides, *z_ways)
        keys = [keys, key_sides[0], *key_far, key_sides[1]]
        values = [values, value_sides[0], *value_far, value_sides[1]]
        return attend(ring_spots, queries, heads[0] * HEAD, keys, values)

    sides_a, sides_b = sides(RING_A), sides(RING_B)
    joint_a = gather_heads(JOINT_A, by_joint(both_a, JOINT_A))
    ring_a = gather_heads(RING_A, by_ring(sides_a, RING_A))
    ring_b = gather_heads(RING_B, by_ring(sides_b, RING_B))
    joint_b = gather_heads(JOINT_B, by_joint(both_late, JOINT_B))
    total = project(hidden, joint_a + ring_a, jnp.float32)
    total = project(total, ring_b, jnp.float32)
    return project(total, joint_b, jnp.bfloat16)


def solution(mesh):
    placed = (
        P("kv", "pb"),
        P("kv", None, "pb"),
        P("kv", None, "pb"),
        P("kv", None),
        P("pb", None),
        P("kv", "pb"),
    )
    return jax.shard_map(
        on_device, mesh=mesh, in_specs=placed, out_specs=P("kv", "pb"), check_vma=False
    )
```

time: 522 us -> 334 us (0.64)
  waiting for transfers between devices: 432 us -> 153 us
  starting transfers between devices: 0.08 us -> 75.2 us
  local copies, waits for them, and re-layouts: 0.01 us -> 32.3 us
  matrix products: 19.8 us -> 0 us
    all_gather x2, waiting for transfers between devices: 318 us -> 0.01 us  [plane_gather(): lax.all_gather(payload, 'kv', axis=0, tiled=True, axis_index_groups=PLANES)]
    ppermute x0 -> x42, waiting for transfers between devices: none -> 153 us  [the longest x8 39.5 us: both_ways(): return (lax.ppermute(line, 'kv', minus), lax.ppermute(line, 'kv', plus))]
    reduce_scatter x1 -> x0, waiting for transfers between devices: 112 us -> none  [on_device(): lax.psum_scatter(partial_value.astype(jnp.bfloat16), 'pb', scatter_dimens...]
    ppermute x0 -> x42, starting transfers between devices: none -> 75.1 us  [the longest x4 10.8 us: gather_heads(): cross = lax.ppermute(near, 'pb', pb_flip(1))]
    slice x0 -> x14, local copies, waits for them, and re-layouts: none -> 20.7 us  [the longest x4 6.93 us: pass_on(): first = lax.ppermute(up[:half], 'kv', minus)]
    dot_general x1 -> x0, matrix products: 19.8 us -> none  [on_device(): jnp.dot(attended, out_weight, preferred_element_type=jnp.float32)]
    unnamed x2 -> x19, local copies, waits for them, and re-layouts: 0.01 us -> 6.56 us
    pallas_call x1 -> x7, Pallas kernels: 52.4 us -> 55.5 us  [the longest x3 28.3 us: project(): pl.pallas_call(project_kernel, out_shape=jax.ShapeDtypeStruct((tok_rows,...]
  transfers between devices with their start and end apart: 3 -> 44, of which waited for: 3 -> 19; matrix products, arithmetic and copies ran while one was open for 0% -> 8% of each run, Pallas kernels for 0% -> 14%
where the time goes in v2:
time: 334 us; the launch traced here: 333 us
  waiting for transfers between devices  153 us (46%)
  starting transfers between devices  75.2 us (23%)
  Pallas kernels  55.5 us (17%)
  local copies, waits for them, and re-layouts  32.3 us (10%)
  between operations  13.6 us (4%)
  other arithmetic  3.51 us (1%)
    ppermute x8, waiting for transfers between devices, both_ways(): return (lax.ppermute(line, 'kv', minus), lax.ppermute(line, 'kv', plus))  39.5 us
    pallas_call x3, Pallas kernels, project(): pl.pallas_call(project_kernel, out_shape=jax.ShapeDtypeStruct((tok_rows,...  28.3 us
    pallas_call x4, Pallas kernels, attend(): pl.pallas_call(functools.partial(attend_kernel, first_col, len(key_parts)...  27.2 us
    ppermute x4, waiting for transfers between devices, gather_heads(): near = lax.ppermute(mine, 'pb', pb_flip(2))  22 us
    ppermute x3, waiting for transfers between devices, swapped(): return jnp.concatenate([own, lax.ppermute(own, 'kv', swap)])  20.1 us
    ppermute x1, waiting for transfers between devices, exchange_weights(): lax.ppermute(send3[:mid], 'pb', pb_flip(3))  19.2 us
    ppermute x4, waiting for transfers between devices, pass_on(): first = lax.ppermute(up[:half], 'kv', minus)  15 us
    ppermute x4, waiting for transfers between devices, pass_on(): second = lax.ppermute(down[half:], 'kv', plus)  13 us
  transfers between devices with their start and end apart: 44, of which 19 were waited for; matrix products, arithmetic and copies ran while one was open for 8% of the time, Pallas kernels for 14%

profile of v2, /device:TPU:1, one launch (start us, length us, event | category | flops | bytes accessed | tf_op | source)
XLA Modules:
  0.0 333.1 jit_solution(122192790020755622)
XLA Ops:
  8.7 3.6 %collective-permute-start = (bf16[2,256,256]{2,1,0:T(8,128)(2,1)S(1)}, bf16[2,256,256]{2,1,0:T(8,128)(2,1)S(1)}, u32[]{:S(2)}, u32[]{:S(2)}) collective-permute-start(bf16[2,256,256]{2,1,0:T(8,128)(2,1)S(1)} %get-tuple-element.30), channel_id=1, source_target_pairs={{0,4},{4,0},{8,12},{12,8},{16,20},{20,16},{24,28},{28,24},{32,36},... | collective-permute-start | bytes 786440 | tf_op jit(solution)/shard_map/ppermute | solution.py:241
  12.4 5.6 %collective-permute-done = bf16[2,256,256]{2,1,0:T(8,128)(2,1)S(1)} collective-permute-done((bf16[2,256,256]{2,1,0:T(8,128)(2,1)S(1)}, bf16[2,256,256]{2,1,0:T(8,128)(2,1)S(1)}, u32[]{:S(2)}, u32[]{:S(2)}) %collective-permute-start) | collective-permute-done | bytes 262176 | tf_op jit(solution)/shard_map/ppermute | solution.py:241
  22.1 4.9 %collective-permute-done.38 = bf16[2,256,256]{2,1,0:T(8,128)(2,1)S(1)} collective-permute-done((bf16[2,256,256]{2,1,0:T(8,128)(2,1)S(1)}, bf16[2,256,256]{2,1,0:T(8,128)(2,1)S(1)}, u32[]{:S(2)}, u32[]{:S(2)}) %collective-permute-start.38) | collective-permute-done | bytes 262176 | tf_op jit(solution)/shard_map/ppermute | solution.py:241
  30.9 9.6 %collective-permute-done.4 = bf16[2,256,512]{2,1,0:T(8,128)(2,1)S(1)} collective-permute-done((bf16[2,256,512]{2,1,0:T(8,128)(2,1)S(1)}, bf16[2,256,512]{2,1,0:T(8,128)(2,1)S(1)}, u32[]{:S(2)}, u32[]{:S(2)}) %collective-permute-start.4) | collective-permute-done | bytes 524320 | tf_op jit(solution)/shard_map/ppermute | solution.py:241
  42.7 3.3 collective-permute-start.6
  50.6 7.5 %collective-permute-done.7 = bf16[2,256,512]{2,1,0:T(8,128)(2,1)S(1)} collective-permute-done((bf16[2,256,512]{2,1,0:T(8,128)(2,1)S(1)}, bf16[2,256,512]{2,1,0:T(8,128)(2,1)S(1)}, u32[]{:S(2)}, u32[]{:S(2)}) %collective-permute-start.7) | collective-permute-done | bytes 524320 | tf_op jit(solution)/shard_map/ppermute | solution.py:173
  59.4 9.2 %collective-permute-done.6 = bf16[2,256,512]{2,1,0:T(8,128)(2,1)S(1)} collective-permute-done((bf16[2,256,512]{2,1,0:T(8,128)(2,1)S(1)}, bf16[2,256,512]{2,1,0:T(8,128)(2,1)S(1)}, u32[]{:S(2)}, u32[]{:S(2)}) %collective-permute-start.6) | collective-permute-done | bytes 524320 | tf_op jit(solution)/shard_map/ppermute | solution.py:174
  68.6 5.5 %collective-permute-done.5 = bf16[2,256,512]{2,1,0:T(8,128)(2,1)S(1)} collective-permute-done((bf16[2,256,512]{2,1,0:T(8,128)(2,1)S(1)}, bf16[2,256,512]{2,1,0:T(8,128)(2,1)S(1)}, u32[]{:S(2)}, u32[]{:S(2)}) %collective-permute-start.5) | collective-permute-done | bytes 524320 | tf_op jit(solution)/shard_map/ppermute | solution.py:172
  77.8 3.2 collective-permute-start.11
  84.2 4.0 %fusion.3 = (bf16[512,1024]{1,0:T(8,128)(2,1)}, bf16[512,1024]{1,0:T(8,128)(2,1)}, bf16[512,1024]{1,0:T(8,128)(2,1)S(1)}, bf16[512,1024]{1,0:T(8,128)(2,1)}) fusion(bf16[1024,4096]{1,0:T(8,128)(2,1)} %param.10, s32[]{:T(128)S(6)} %add.329, s32[]{:T(128)S(6)} %select_n.293, s32[]{:T(128)S(6)} %select_n.292), kind=kLoop, calls=%fused_computation.60 | loop fusion | bytes 8388620 | tf_op jit(solution)/shard_map/slice | solution.py:207
  89.3 35.8 %collective-permute-done.11.refs_1_ = bf16[8,256,256]{2,1,0:T(8,128)(2,1)S(1)} collective-permute-done((bf16[8,256,256]{2,1,0:T(8,128)(2,1)S(1)}, bf16[8,256,256]{2,1,0:T(8,128)(2,1)S(1)}, u32[]{:S(2)}, u32[]{:S(2)}) %collective-permute-start.11) | collective-permute-done | bytes 1048608 | tf_op jit(solution)/shard_map/ppermute | solution.py:184
  126.1 6.4 %collective-permute-start.24 = (bf16[512,1024]{1,0:T(8,128)(2,1)}, bf16[512,1024]{1,0:T(8,128)(2,1)S(1)}, u32[]{:S(2)}, u32[]{:S(2)}) collective-permute-start(bf16[512,1024]{1,0:T(8,128)(2,1)} %get-tuple-element.20), channel_id=1, source_target_pairs={{0,3},{1,2},{2,1},{3,0},{4,7},{5,6},{6,5},{7,4},{8,11},{9,10},{10,... | collective-permute-start | bytes 3145736 | tf_op jit(solution)/shard_map/ppermute | solution.py:206
  137.5 19.2 %collective-permute-done.24.refs_11_.refs_15_ = bf16[512,1024]{1,0:T(8,128)(2,1)S(1)} collective-permute-done((bf16[512,1024]{1,0:T(8,128)(2,1)}, bf16[512,1024]{1,0:T(8,128)(2,1)S(1)}, u32[]{:S(2)}, u32[]{:S(2)}) %collective-permute-start.24) | collective-permute-done | bytes 1048608 | tf_op jit(solution)/shard_map/ppermute | solution.py:206
  160.1 4.0 %constant_dynamic-slice_fusion.2 = (bf16[1024,1024]{1,0:T(8,128)(2,1)}, bf16[1024,1024]{1,0:T(8,128)(2,1)S(1)}) fusion(bf16[1024,4096]{1,0:T(8,128)(2,1)} %param.10, s32[]{:T(128)S(6)} %select_n.291, s32[]{:T(128)S(6)} %select_n.290), kind=kLoop, calls=%fused_computation.46 | loop fusion | bytes 8388616 | tf_op jit(solution)/shard_map/dynamic_slice | solution.py:253
  177.7 6.9 %collective-permute-done.12.refs_2_ = bf16[4,256,256]{2,1,0:T(8,128)(2,1)} collective-permute-done((bf16[4,256,256]{2,1,0:T(8,128)(2,1)S(1)}, bf16[4,256,256]{2,1,0:T(8,128)(2,1)}, u32[]{:S(2)}, u32[]{:S(2)}) %collective-permute-start.12) | collective-permute-done | bytes 524320 | tf_op jit(solution)/shard_map/ppermute | solution.py:189
  184.6 3.5 %collective-permute-start.26 = (bf16[4,256,256]{2,1,0:T(8,128)(2,1)}, bf16[4,256,256]{2,1,0:T(8,128)(2,1)}, u32[]{:S(2)}, u32[]{:S(2)}) collective-permute-start(bf16[4,256,256]{2,1,0:T(8,128)(2,1)} %slice.90), channel_id=1, source_target_pairs={{0,96},{4,100},{8,104},{12,108},{16,112},{20,116},{24,120},{28,124... | collective-permute-start | bytes 1572872 | tf_op jit(solution)/shard_map/ppermute | solution.py:189
  189.3 6.8 %collective-permute-done.14.refs_3_ = bf16[4,256,256]{2,1,0:T(8,128)(2,1)} collective-permute-done((bf16[4,256,256]{2,1,0:T(8,128)(2,1)}, bf16[4,256,256]{2,1,0:T(8,128)(2,1)}, u32[]{:S(2)}, u32[]{:S(2)}) %collective-permute-start.14) | collective-permute-done | bytes 524320 | tf_op jit(solution)/shard_map/ppermute | solution.py:190
  203.0 8.1 %collective-permute-done.26.refs_2_ = bf16[4,256,256]{2,1,0:T(8,128)(2,1)} collective-permute-done((bf16[4,256,256]{2,1,0:T(8,128)(2,1)}, bf16[4,256,256]{2,1,0:T(8,128)(2,1)}, u32[]{:S(2)}, u32[]{:S(2)}) %collective-permute-start.26) | collective-permute-done | bytes 524320 | tf_op jit(solution)/shard_map/ppermute | solution.py:189
  211.7 6.8 %attend.5.refs_4_ = bf16[1536,256]{1,0:T(8,128)(2,1)} custom-call(s32[4,24]{1,0:T(4,128)} %pad_add_fusion.1.spot_ref, bf16[1536,1024]{1,0:T(8,128)(2,1)} %q_hbm.7, bf16[8,256,256]{2,1,0:T(8,128)(2,1)} %copy-done.6, bf16[8,256,256]{2,1,0:T(8,128)(2,1)} %copy-done.7, bf16[4,256,256]{2,1,0:T(8,128)(2,1)} %collective-permute-done.12.refs_2_, ...), custom_call_target="tpu_custom_call" | custom-call | flops 402653184 | bytes 20971520 | tf_op jit(solution)/shard_map/attend/pallas_call | solution.py:113
  218.5 5.2 %collective-permute-done.28.refs_3_ = bf16[4,256,256]{2,1,0:T(8,128)(2,1)} collective-permute-done((bf16[4,256,256]{2,1,0:T(8,128)(2,1)S(1)}, bf16[4,256,256]{2,1,0:T(8,128)(2,1)}, u32[]{:S(2)}, u32[]{:S(2)}) %collective-permute-start.28) | collective-permute-done | bytes 524320 | tf_op jit(solution)/shard_map/ppermute | solution.py:190
  225.6 6.8 %attend.4.refs_0_ = bf16[1536,256]{1,0:T(8,128)(2,1)} custom-call(s32[4,24]{1,0:T(4,128)} %pad_add_fusion.spot_ref, bf16[1536,1024]{1,0:T(8,128)(2,1)} %q_hbm.7, bf16[64,256,256]{2,1,0:T(8,128)(2,1)} %all-gather.3.cloned.1.call-done.refs_0_.refs_1_, bf16[64,256,256]{2,1,0:T(8,128)(2,1)} %all-gather.3.cloned.1.call-done.refs_0_.refs_1_), custom_call_target="tpu_custom_call" | custom-call | flops 402653184 | bytes 20971520 | tf_op jit(solution)/shard_map/attend/pallas_call | solution.py:113
  235.4 6.8 %attend.6.refs_0_ = bf16[1536,256]{1,0:T(8,128)(2,1)} custom-call(s32[4,24]{1,0:T(4,128)} %pad_add_fusion.1.spot_ref, bf16[1536,1024]{1,0:T(8,128)(2,1)} %q_hbm.7, bf16[8,256,256]{2,1,0:T(8,128)(2,1)} %get-tuple-element.27.refs_0_, bf16[8,256,256]{2,1,0:T(8,128)(2,1)} %collective-permute-done.25.refs_1_, ...), custom_call_target="tpu_custom_call" | custom-call | flops 402653184 | bytes 20971520 | tf_op jit(solution)/shard_map/attend/pallas_call | solution.py:113
  242.9 4.0 %collective-permute-start.21 = (bf16[1536,256]{1,0:T(8,128)(2,1)}, bf16[1536,256]{1,0:T(8,128)(2,1)}, u32[]{:S(2)}, u32[]{:S(2)}) collective-permute-start(bf16[1536,256]{1,0:T(8,128)(2,1)} %collective-permute-done.20.refs_6_), channel_id=1, source_target_pairs={{0,1},{1,0},{2,3},{3,2},{4,5},{5,4},{6,7},{7,6},{8,9},{9,8},{10,11... | collective-permute-start | bytes 2359304 | tf_op jit(solution)/shard_map/ppermute | solution.py:265
  246.9 6.8 %attend.7.refs_0_ = bf16[1536,256]{1,0:T(8,128)(2,1)} custom-call(s32[4,24]{1,0:T(4,128)} %pad_add_fusion.spot_ref, bf16[1536,1024]{1,0:T(8,128)(2,1)} %q_hbm.7, bf16[64,256,256]{2,1,0:T(8,128)(2,1)} %all-gather.5.cloned.1.call-done.refs_0_.refs_1_, bf16[64,256,256]{2,1,0:T(8,128)(2,1)} %all-gather.5.cloned.1.call-done.refs_0_.refs_1_), custom_call_target="tpu_custom_call" | custom-call | flops 402653184 | bytes 20971520 | tf_op jit(solution)/shard_map/attend/pallas_call | solution.py:113
  257.5 6.2 %collective-permute-start.3 = (bf16[1536,256]{1,0:T(8,128)(2,1)}, bf16[1536,256]{1,0:T(8,128)(2,1)S(1)}, u32[]{:S(2)}, u32[]{:S(2)}) collective-permute-start(bf16[1536,256]{1,0:T(8,128)(2,1)} %collective-permute-done.2.refs_2_), channel_id=1, source_target_pairs={{0,1},{1,0},{2,3},{3,2},{4,5},{5,4},{6,7},{7,6},{8,9},{9,8},{10,11... | collective-permute-start | bytes 2359304 | tf_op jit(solution)/shard_map/ppermute | solution.py:265
  263.8 10.6 %collective-permute-done.34.refs_2_ = bf16[1536,256]{1,0:T(8,128)(2,1)} collective-permute-done((bf16[1536,256]{1,0:T(8,128)(2,1)}, bf16[1536,256]{1,0:T(8,128)(2,1)}, u32[]{:S(2)}, u32[]{:S(2)}) %collective-permute-start.34) | collective-permute-done | bytes 786464 | tf_op jit(solution)/shard_map/ppermute | solution.py:264
  274.4 8.0 %collective-permute-start.37 = (bf16[512,1024]{1,0:T(8,128)(2,1)}, bf16[512,1024]{1,0:T(8,128)(2,1)S(1)}, u32[]{:S(2)}, u32[]{:S(2)}) collective-permute-start(bf16[512,1024]{1,0:T(8,128)(2,1)} %get-tuple-element.19), channel_id=1, source_target_pairs={{0,7},{1,6},{2,5},{3,4},{4,3},{5,2},{6,1},{7,0},{8,15},{9,14},{10,... | collective-permute-start | bytes 3145736 | tf_op jit(solution)/shard_map/ppermute | solution.py:207
  282.9 8.2 %collective-permute-done.40.refs_2_ = bf16[1536,256]{1,0:T(8,128)(2,1)S(1)} collective-permute-done((bf16[1536,256]{1,0:T(8,128)(2,1)}, bf16[1536,256]{1,0:T(8,128)(2,1)S(1)}, u32[]{:S(2)}, u32[]{:S(2)}) %collective-permute-start.40) | collective-permute-done | bytes 786464 | tf_op jit(solution)/shard_map/ppermute | solution.py:264
  291.1 3.3 collective-permute-start.39
  297.9 11.2 %shard_map.64.base_ref = f32[1536,1024]{1,0:T(8,128)} custom-call(bf16[1536,1024]{1,0:T(8,128)(2,1)} %base_ref.1, bf16[1536,256]{1,0:T(8,128)(2,1)S(1)} %copy-done.3, bf16[1536,256]{1,0:T(8,128)(2,1)} %collective-permute-done.1.refs_1_, bf16[1536,256]{1,0:T(8,128)(2,1)} %collective-permute-done.2.refs_2_, ...), custom_call_target="tpu_custom_call" | custom-call | flops 6442450944 | bytes 20971520 | tf_op jit(solution)/shard_map/pallas_call | solution.py:156
  309.1 8.9 %shard_map.65.base_ref = f32[1536,1024]{1,0:T(8,128)} custom-call(f32[1536,1024]{1,0:T(8,128)} %shard_map.64.base_ref, bf16[1536,256]{1,0:T(8,128)(2,1)S(1)} %copy-done.4, bf16[1536,256]{1,0:T(8,128)(2,1)S(1)} %collective-permute-done.33.refs_1_, bf16[1536,256]{1,0:T(8,128)(2,1)} %collective-permute-done.34.refs_2_, ...), custom_call_target="tpu_custom_call" | custom-call | flops 3221225472 | bytes 20971520 | tf_op jit(solution)/shard_map/pallas_call | solution.py:156
  318.1 8.2 %shard_map.66 = bf16[1536,1024]{1,0:T(8,128)(2,1)} custom-call(f32[1536,1024]{1,0:T(8,128)} %shard_map.65.base_ref, bf16[1536,256]{1,0:T(8,128)(2,1)S(1)} %copy-done.5, bf16[1536,256]{1,0:T(8,128)(2,1)S(1)} %collective-permute-done.39.refs_1_, bf16[1536,256]{1,0:T(8,128)(2,1)S(1)} %collective-permute-done.40.refs_2_, ...), custom_call_target="tpu_custom_call" | custom-call | flops 3221225472 | bytes 20971520 | tf_op jit(solution)/shard_map/pallas_call | solution.py:156
  (111 shorter events, 71.2 us)
Async XLA Ops:
  6.5 219.0 %all-gather.3.cloned.1.call-start = ((), (), s32[]{:S(2)}) async-start(), calls=%async_computation | async-start | bytes 8912896 | tf_op jit(solution)/shard_map/all_gather | solution.py:195
  18.9 228.1 %all-gather.5.cloned.1.call-start = ((), (), s32[]{:S(2)}) async-start(), calls=%async_computation.1 | async-start | bytes 8912896 | tf_op jit(solution)/shard_map/all_gather | solution.py:195
  46.0 28.1 %collective-permute-start.5 = (bf16[2,256,512]{2,1,0:T(8,128)(2,1)S(1)}, bf16[2,256,512]{2,1,0:T(8,128)(2,1)S(1)}, u32[]{:S(2)}, u32[]{:S(2)}) collective-permute-start(bf16[2,256,512]{2,1,0:T(8,128)(2,1)S(1)} %get-tuple-element.32), channel_id=1, source_target_pairs={{0,24},{4,28},{8,0},{12,4},{16,8},{20,12},{24,16},{28,20},{32,56},... | collective-permute-start | bytes 1572872 | tf_op jit(solution)/shard_map/ppermute | solution.py:172
  46.7 27.7 %collective-permute-start.10 = (bf16[2,256,512]{2,1,0:T(8,128)(2,1)S(1)}, bf16[2,256,512]{2,1,0:T(8,128)(2,1)S(1)}, u32[]{:S(2)}, u32[]{:S(2)}) collective-permute-start(bf16[2,256,512]{2,1,0:T(8,128)(2,1)S(1)} %get-tuple-element.31), channel_id=1, source_target_pairs={{0,32},{4,36},{8,40},{12,44},{16,48},{20,52},{24,56},{28,60},{32,6... | collective-permute-start | bytes 1572872 | tf_op jit(solution)/shard_map/ppermute | solution.py:173
  48.0 26.4 %collective-permute-start.9 = (bf16[2,256,512]{2,1,0:T(8,128)(2,1)S(1)}, bf16[2,256,512]{2,1,0:T(8,128)(2,1)S(1)}, u32[]{:S(2)}, u32[]{:S(2)}) collective-permute-start(bf16[2,256,512]{2,1,0:T(8,128)(2,1)S(1)} %get-tuple-element.31), channel_id=1, source_target_pairs={{0,64},{4,68},{8,72},{12,76},{16,80},{20,84},{24,88},{28,92},{32,9... | collective-permute-start | bytes 1572872 | tf_op jit(solution)/shard_map/ppermute | solution.py:174
  77.8 47.3 %collective-permute-start.11 = (bf16[8,256,256]{2,1,0:T(8,128)(2,1)S(1)}, bf16[8,256,256]{2,1,0:T(8,128)(2,1)S(1)}, u32[]{:S(2)}, u32[]{:S(2)}) collective-permute-start(bf16[8,256,256]{2,1,0:T(8,128)(2,1)S(1)} %get-tuple-element.28.refs_0_), channel_id=1, source_target_pairs={{0,96},{4,100},{8,104},{12,108},{16,112},{20,116},{24,120},{28,124... | collective-permute-start | bytes 3145736 | tf_op jit(solution)/shard_map/ppermute | solution.py:184
  81.0 51.5 %collective-permute-start.13 = (bf16[8,256,256]{2,1,0:T(8,128)(2,1)S(1)}, bf16[8,256,256]{2,1,0:T(8,128)(2,1)}, u32[]{:S(2)}, u32[]{:S(2)}) collective-permute-start(bf16[8,256,256]{2,1,0:T(8,128)(2,1)S(1)} %get-tuple-element.28.refs_0_), channel_id=1, source_target_pairs={{0,32},{4,36},{8,40},{12,44},{16,48},{20,52},{24,56},{28,60},{32,6... | collective-permute-start | bytes 3145736 | tf_op jit(solution)/shard_map/ppermute | solution.py:184
  82.7 52.2 %collective-permute-start.15 = (bf16[8,256,256]{2,1,0:T(8,128)(2,1)}, bf16[8,256,256]{2,1,0:T(8,128)(2,1)}, u32[]{:S(2)}, u32[]{:S(2)}) collective-permute-start(bf16[8,256,256]{2,1,0:T(8,128)(2,1)} %get-tuple-element.26.refs_5_), channel_id=1, source_target_pairs={{0,24},{4,28},{8,0},{12,4},{16,8},{20,12},{24,16},{28,20},{32,56},... | collective-permute-start | bytes 3145736 | tf_op jit(solution)/shard_map/ppermute | solution.py:184
  82.7 52.2 %collective-permute-start.17 = (bf16[8,256,256]{2,1,0:T(8,128)(2,1)}, bf16[8,256,256]{2,1,0:T(8,128)(2,1)}, u32[]{:S(2)}, u32[]{:S(2)}) collective-permute-start(bf16[8,256,256]{2,1,0:T(8,128)(2,1)} %get-tuple-element.26.refs_5_), channel_id=1, source_target_pairs={{0,8},{4,12},{8,16},{12,20},{16,24},{20,28},{24,0},{28,4},{32,40},... | collective-permute-start | bytes 3145736 | tf_op jit(solution)/shard_map/ppermute | solution.py:184
  88.1 47.1 %collective-permute-start.23 = (bf16[512,1024]{1,0:T(8,128)(2,1)S(1)}, bf16[512,1024]{1,0:T(8,128)(2,1)S(1)}, u32[]{:S(2)}, u32[]{:S(2)}) collective-permute-start(bf16[512,1024]{1,0:T(8,128)(2,1)S(1)} %get-tuple-element.21), channel_id=1, source_target_pairs={{0,2},{1,3},{2,0},{3,1},{4,6},{5,7},{6,4},{7,5},{8,10},{9,11},{10,... | collective-permute-start | bytes 3145736 | tf_op jit(solution)/shard_map/ppermute | solution.py:202
  126.1 30.6 %collective-permute-start.24 = (bf16[512,1024]{1,0:T(8,128)(2,1)}, bf16[512,1024]{1,0:T(8,128)(2,1)S(1)}, u32[]{:S(2)}, u32[]{:S(2)}) collective-permute-start(bf16[512,1024]{1,0:T(8,128)(2,1)} %get-tuple-element.20), channel_id=1, source_target_pairs={{0,3},{1,2},{2,1},{3,0},{4,7},{5,6},{6,5},{7,4},{8,11},{9,10},{10,... | collective-permute-start | bytes 3145736 | tf_op jit(solution)/shard_map/ppermute | solution.py:206
  132.5 34.6 %collective-permute-start.25 = (bf16[8,256,256]{2,1,0:T(8,128)(2,1)}, bf16[8,256,256]{2,1,0:T(8,128)(2,1)}, u32[]{:S(2)}, u32[]{:S(2)}) collective-permute-start(bf16[8,256,256]{2,1,0:T(8,128)(2,1)} %get-tuple-element.27.refs_0_), channel_id=1, source_target_pairs={{0,96},{4,100},{8,104},{12,108},{16,112},{20,116},{24,120},{28,124... | collective-permute-start | bytes 3145736 | tf_op jit(solution)/shard_map/ppermute | solution.py:184
  134.9 34.7 %collective-permute-start.27 = (bf16[8,256,256]{2,1,0:T(8,128)(2,1)}, bf16[8,256,256]{2,1,0:T(8,128)(2,1)}, u32[]{:S(2)}, u32[]{:S(2)}) collective-permute-start(bf16[8,256,256]{2,1,0:T(8,128)(2,1)} %get-tuple-element.27.refs_0_), channel_id=1, source_target_pairs={{0,32},{4,36},{8,40},{12,44},{16,48},{20,52},{24,56},{28,60},{32,6... | collective-permute-start | bytes 3145736 | tf_op jit(solution)/shard_map/ppermute | solution.py:184
  134.9 37.6 %collective-permute-start.29 = (bf16[8,256,256]{2,1,0:T(8,128)(2,1)}, bf16[8,256,256]{2,1,0:T(8,128)(2,1)}, u32[]{:S(2)}, u32[]{:S(2)}) collective-permute-start(bf16[8,256,256]{2,1,0:T(8,128)(2,1)} %get-tuple-element.25.refs_5_), channel_id=1, source_target_pairs={{0,24},{4,28},{8,0},{12,4},{16,8},{20,12},{24,16},{28,20},{32,56},... | collective-permute-start | bytes 3145736 | tf_op jit(solution)/shard_map/ppermute | solution.py:184
  135.2 41.0 %collective-permute-start.31 = (bf16[8,256,256]{2,1,0:T(8,128)(2,1)}, bf16[8,256,256]{2,1,0:T(8,128)(2,1)}, u32[]{:S(2)}, u32[]{:S(2)}) collective-permute-start(bf16[8,256,256]{2,1,0:T(8,128)(2,1)} %get-tuple-element.25.refs_5_), channel_id=1, source_target_pairs={{0,8},{4,12},{8,16},{12,20},{16,24},{20,28},{24,0},{28,4},{32,40},... | collective-permute-start | bytes 3145736 | tf_op jit(solution)/shard_map/ppermute | solution.py:184
  157.6 27.0 %collective-permute-start.12 = (bf16[4,256,256]{2,1,0:T(8,128)(2,1)S(1)}, bf16[4,256,256]{2,1,0:T(8,128)(2,1)}, u32[]{:S(2)}, u32[]{:S(2)}) collective-permute-start(bf16[4,256,256]{2,1,0:T(8,128)(2,1)S(1)} %slice.86), channel_id=1, source_target_pairs={{0,96},{4,100},{8,104},{12,108},{16,112},{20,116},{24,120},{28,124... | collective-permute-start | bytes 1572872 | tf_op jit(solution)/shard_map/ppermute | solution.py:189
  167.1 79.8 %collective-permute-start.22 = (bf16[1024,1024]{1,0:T(8,128)(2,1)}, bf16[1024,1024]{1,0:T(8,128)(2,1)}, u32[]{:S(2)}, u32[]{:S(2)}) collective-permute-start(bf16[1024,1024]{1,0:T(8,128)(2,1)} %get-tuple-element.23), channel_id=1, source_target_pairs={{0,1},{1,0},{2,3},{3,2},{4,5},{5,4},{6,7},{7,6},{8,9},{9,8},{10,11... | collective-permute-start | bytes 6291464 | tf_op jit(solution)/shard_map/ppermute | solution.py:199
  169.6 26.5 %collective-permute-start.14 = (bf16[4,256,256]{2,1,0:T(8,128)(2,1)}, bf16[4,256,256]{2,1,0:T(8,128)(2,1)}, u32[]{:S(2)}, u32[]{:S(2)}) collective-permute-start(bf16[4,256,256]{2,1,0:T(8,128)(2,1)} %slice.87), channel_id=1, source_target_pairs={{0,32},{4,36},{8,40},{12,44},{16,48},{20,52},{24,56},{28,60},{32,6... | collective-permute-start | bytes 1572872 | tf_op jit(solution)/shard_map/ppermute | solution.py:190
  176.3 26.4 %collective-permute-start.18 = (bf16[4,256,256]{2,1,0:T(8,128)(2,1)}, bf16[4,256,256]{2,1,0:T(8,128)(2,1)}, u32[]{:S(2)}, u32[]{:S(2)}) collective-permute-start(bf16[4,256,256]{2,1,0:T(8,128)(2,1)} %slice.89), channel_id=1, source_target_pairs={{0,8},{4,12},{8,16},{12,20},{16,24},{20,28},{24,0},{28,4},{32,40},... | collective-permute-start | bytes 1572872 | tf_op jit(solution)/shard_map/ppermute | solution.py:190
  184.6 26.4 %collective-permute-start.26 = (bf16[4,256,256]{2,1,0:T(8,128)(2,1)}, bf16[4,256,256]{2,1,0:T(8,128)(2,1)}, u32[]{:S(2)}, u32[]{:S(2)}) collective-permute-start(bf16[4,256,256]{2,1,0:T(8,128)(2,1)} %slice.90), channel_id=1, source_target_pairs={{0,96},{4,100},{8,104},{12,108},{16,112},{20,116},{24,120},{28,124... | collective-permute-start | bytes 1572872 | tf_op jit(solution)/shard_map/ppermute | solution.py:189
  196.1 46.1 %collective-permute-start.36 = (bf16[512,1024]{1,0:T(8,128)(2,1)}, bf16[512,1024]{1,0:T(8,128)(2,1)}, u32[]{:S(2)}, u32[]{:S(2)}) collective-permute-start(bf16[512,1024]{1,0:T(8,128)(2,1)} %get-tuple-element.22), channel_id=1, source_target_pairs={{0,6},{1,7},{2,4},{3,5},{4,2},{5,3},{6,0},{7,1},{8,14},{9,15},{10,... | collective-permute-start | bytes 3145736 | tf_op jit(solution)/shard_map/ppermute | solution.py:203
  197.8 25.9 %collective-permute-start.28 = (bf16[4,256,256]{2,1,0:T(8,128)(2,1)S(1)}, bf16[4,256,256]{2,1,0:T(8,128)(2,1)}, u32[]{:S(2)}, u32[]{:S(2)}) collective-permute-start(bf16[4,256,256]{2,1,0:T(8,128)(2,1)S(1)} %slice.91), channel_id=1, source_target_pairs={{0,32},{4,36},{8,40},{12,44},{16,48},{20,52},{24,56},{28,60},{32,6... | collective-permute-start | bytes 1572872 | tf_op jit(solution)/shard_map/ppermute | solution.py:190
  202.7 29.7 %collective-permute-start.30 = (bf16[4,256,256]{2,1,0:T(8,128)(2,1)}, bf16[4,256,256]{2,1,0:T(8,128)(2,1)}, u32[]{:S(2)}, u32[]{:S(2)}) collective-permute-start(bf16[4,256,256]{2,1,0:T(8,128)(2,1)} %slice.92), channel_id=1, source_target_pairs={{0,24},{4,28},{8,0},{12,4},{16,8},{20,12},{24,16},{28,20},{32,56},... | collective-permute-start | bytes 1572872 | tf_op jit(solution)/shard_map/ppermute | solution.py:189
  242.2 32.2 %collective-permute-start.34 = (bf16[1536,256]{1,0:T(8,128)(2,1)}, bf16[1536,256]{1,0:T(8,128)(2,1)}, u32[]{:S(2)}, u32[]{:S(2)}) collective-permute-start(bf16[1536,256]{1,0:T(8,128)(2,1)} %attend.6.refs_0_), channel_id=1, source_target_pairs={{0,2},{1,3},{2,0},{3,1},{4,6},{5,7},{6,4},{7,5},{8,10},{9,11},{10,... | collective-permute-start | bytes 2359304 | tf_op jit(solution)/shard_map/ppermute | solution.py:264
  242.9 39.5 %collective-permute-start.21 = (bf16[1536,256]{1,0:T(8,128)(2,1)}, bf16[1536,256]{1,0:T(8,128)(2,1)}, u32[]{:S(2)}, u32[]{:S(2)}) collective-permute-start(bf16[1536,256]{1,0:T(8,128)(2,1)} %collective-permute-done.20.refs_6_), channel_id=1, source_target_pairs={{0,1},{1,0},{2,3},{3,2},{4,5},{5,4},{6,7},{7,6},{8,9},{9,8},{10,11... | collective-permute-start | bytes 2359304 | tf_op jit(solution)/shard_map/ppermute | solution.py:265
  246.9 35.5 %collective-permute-start.1 = (bf16[1536,256]{1,0:T(8,128)(2,1)}, bf16[1536,256]{1,0:T(8,128)(2,1)}, u32[]{:S(2)}, u32[]{:S(2)}) collective-permute-start(bf16[1536,256]{1,0:T(8,128)(2,1)} %attend.4.refs_0_), channel_id=1, source_target_pairs={{0,1},{1,0},{2,3},{3,2},{4,5},{5,4},{6,7},{7,6},{8,9},{9,8},{10,11... | collective-permute-start | bytes 2359304 | tf_op jit(solution)/shard_map/ppermute | solution.py:263
  253.7 37.4 %collective-permute-start.40 = (bf16[1536,256]{1,0:T(8,128)(2,1)}, bf16[1536,256]{1,0:T(8,128)(2,1)S(1)}, u32[]{:S(2)}, u32[]{:S(2)}) collective-permute-start(bf16[1536,256]{1,0:T(8,128)(2,1)} %attend.7.refs_0_), channel_id=1, source_target_pairs={{0,2},{1,3},{2,0},{3,1},{4,6},{5,7},{6,4},{7,5},{8,10},{9,11},{10,... | collective-permute-start | bytes 2359304 | tf_op jit(solution)/shard_map/ppermute | solution.py:264
  257.5 36.9 %collective-permute-start.3 = (bf16[1536,256]{1,0:T(8,128)(2,1)}, bf16[1536,256]{1,0:T(8,128)(2,1)S(1)}, u32[]{:S(2)}, u32[]{:S(2)}) collective-permute-start(bf16[1536,256]{1,0:T(8,128)(2,1)} %collective-permute-done.2.refs_2_), channel_id=1, source_target_pairs={{0,1},{1,0},{2,3},{3,2},{4,5},{5,4},{6,7},{7,6},{8,9},{9,8},{10,11... | collective-permute-start | bytes 2359304 | tf_op jit(solution)/shard_map/ppermute | solution.py:265
  274.4 34.7 %collective-permute-start.37 = (bf16[512,1024]{1,0:T(8,128)(2,1)}, bf16[512,1024]{1,0:T(8,128)(2,1)S(1)}, u32[]{:S(2)}, u32[]{:S(2)}) collective-permute-start(bf16[512,1024]{1,0:T(8,128)(2,1)} %get-tuple-element.19), channel_id=1, source_target_pairs={{0,7},{1,6},{2,5},{3,4},{4,3},{5,2},{6,1},{7,0},{8,15},{9,14},{10,... | collective-permute-start | bytes 3145736 | tf_op jit(solution)/shard_map/ppermute | solution.py:207
  282.4 26.8 %collective-permute-start.33 = (bf16[1536,256]{1,0:T(8,128)(2,1)}, bf16[1536,256]{1,0:T(8,128)(2,1)S(1)}, u32[]{:S(2)}, u32[]{:S(2)}) collective-permute-start(bf16[1536,256]{1,0:T(8,128)(2,1)} %attend.6.refs_0_), channel_id=1, source_target_pairs={{0,1},{1,0},{2,3},{3,2},{4,5},{5,4},{6,7},{7,6},{8,9},{9,8},{10,11... | collective-permute-start | bytes 2359304 | tf_op jit(solution)/shard_map/ppermute | solution.py:263
  282.4 26.8 %collective-permute-start.35 = (bf16[1536,256]{1,0:T(8,128)(2,1)}, bf16[1536,256]{1,0:T(8,128)(2,1)S(1)}, u32[]{:S(2)}, u32[]{:S(2)}) collective-permute-start(bf16[1536,256]{1,0:T(8,128)(2,1)} %collective-permute-done.34.refs_2_), channel_id=1, source_target_pairs={{0,1},{1,0},{2,3},{3,2},{4,5},{5,4},{6,7},{7,6},{8,9},{9,8},{10,11... | collective-permute-start | bytes 2359304 | tf_op jit(solution)/shard_map/ppermute | solution.py:265
  291.1 27.0 %collective-permute-start.39 = (bf16[1536,256]{1,0:T(8,128)(2,1)}, bf16[1536,256]{1,0:T(8,128)(2,1)S(1)}, u32[]{:S(2)}, u32[]{:S(2)}) collective-permute-start(bf16[1536,256]{1,0:T(8,128)(2,1)} %attend.7.refs_0_), channel_id=1, source_target_pairs={{0,1},{1,0},{2,3},{3,2},{4,5},{5,4},{6,7},{7,6},{8,9},{9,8},{10,11... | collective-permute-start | bytes 2359304 | tf_op jit(solution)/shard_map/ppermute | solution.py:263
  (21 other events, 279.1 us)
Sparse Core Ops, SparseCore 0:
  19.0 109.4 all-gather.2
  130.6 98.9 all-gather.4

commit v3 on v2

--- a/solution.py
+++ b/solution.py
@@ -126,7 +126,7 @@
                 pltpu.SemaphoreType.DMA,
             ],
         ),
-        compiler_params=pltpu.CompilerParams(vmem_limit_bytes=60 << 20),
+        compiler_params=pltpu.CompilerParams(vmem_limit_bytes=63 << 20),
         cost_estimate=pl.CostEstimate(
             flops=flops, bytes_accessed=20 << 20, transcendentals=0
         ),
@@ -161,7 +161,7 @@
         + [pl.BlockSpec((rows, part.shape[1]), lambda i: (i, 0)) for part in features]
         + [held(part.shape[1], place) for part, _, place in pairs],
         out_specs=wide,
-        compiler_params=pltpu.CompilerParams(vmem_limit_bytes=40 << 20),
+        compiler_params=pltpu.CompilerParams(vmem_limit_bytes=63 << 20),
         cost_estimate=pl.CostEstimate(
             flops=2 * tok_rows * depth * out_width, bytes_accessed=20 << 20, transcendentals=0
         ),
@@ -294,8 +294,8 @@
     ring_b = gather_heads(RING_B, by_ring(sides_b, RING_B))
     joint_b = gather_heads(JOINT_B, by_joint(both_late, JOINT_B))
     total = project(hidden, joint_a + ring_a, jnp.float32)
-    total = project(total, ring_b, jnp.float32)
-    return project(total, joint_b, jnp.bfloat16)
+    total = project(total, ring_b + joint_b[:2], jnp.float32)
+    return project(total, joint_b[2:], jnp.bfloat16)
 
 
 def solution(mesh):

time: 334 us -> 348 us (1.042)
  starting transfers between devices: 75.2 us -> 97 us
  local copies, waits for them, and re-layouts: 32.3 us -> 19.7 us
  Pallas kernels: 55.5 us -> 59 us
    ppermute x8, waiting for transfers between devices: 39.5 us -> 56.5 us  [both_ways(): return (lax.ppermute(line, 'kv', minus), lax.ppermute(line, 'kv', plus))]
    ppermute x4, starting transfers between devices: 10.8 us -> 23.9 us  [gather_heads(): cross = lax.ppermute(near, 'pb', pb_flip(1))]
    ppermute x1, waiting for transfers between devices: 19.2 us -> 7.02 us  [exchange_weights(): lax.ppermute(send3[:mid], 'pb', pb_flip(3))]
    ppermute x2, waiting for transfers between devices: 7.54 us -> 19.5 us  [near_ring(): down = lax.ppermute(block, 'kv', plus)]
    ppermute x4, waiting for transfers between devices: 15 us -> 5.97 us  [pass_on(): first = lax.ppermute(up[:half], 'kv', minus)]
    ppermute x2, waiting for transfers between devices: 9.23 us -> 18.1 us  [near_ring(): far = lax.ppermute(block, 'kv', twice(minus))]
    ppermute x1, starting transfers between devices: 0.01 us -> 8.79 us  [exchange_weights(): core = lax.ppermute(columns(pb ^ 1), 'pb', pb_flip(1))]
    ppermute x4, waiting for transfers between devices: 13 us -> 4.53 us  [pass_on(): second = lax.ppermute(down[half:], 'kv', plus)]
  transfers between devices with their start and end apart: 44 -> 44, of which waited for: 19 -> 18; matrix products, arithmetic and copies ran while one was open for 8% -> 6% of each run, Pallas kernels for 14% -> 15%
where the time goes in v3:
time: 348 us; the launch traced here: 347 us
  waiting for transfers between devices  154 us (44%)
  starting transfers between devices  97 us (28%)
  Pallas kernels  59 us (17%)
  local copies, waits for them, and re-layouts  19.7 us (6%)
  between operations  13.7 us (4%)
  other arithmetic  3.56 us (1%)
    ppermute x8, waiting for transfers between devices, both_ways(): return (lax.ppermute(line, 'kv', minus), lax.ppermute(line, 'kv', plus))  56.5 us
    pallas_call x3, Pallas kernels, project(): pl.pallas_call(project_kernel, out_shape=jax.ShapeDtypeStruct((tok_rows,...  31.8 us
    pallas_call x4, Pallas kernels, attend(): pl.pallas_call(functools.partial(attend_kernel, first_col, len(key_parts)...  27.3 us
    ppermute x4, starting transfers between devices, gather_heads(): cross = lax.ppermute(near, 'pb', pb_flip(1))  23.9 us
    ppermute x3, waiting for transfers between devices, swapped(): return jnp.concatenate([own, lax.ppermute(own, 'kv', swap)])  20.1 us
    ppermute x2, waiting for transfers between devices, near_ring(): down = lax.ppermute(block, 'kv', plus)  19.5 us
    ppermute x4, waiting for transfers between devices, gather_heads(): near = lax.ppermute(mine, 'pb', pb_flip(2))  18.7 us
    ppermute x2, waiting for transfers between devices, near_ring(): far = lax.ppermute(block, 'kv', twice(minus))  18.1 us
  transfers between devices with their start and end apart: 44, of which 18 were waited for; matrix products, arithmetic and copies ran while one was open for 6% of the time, Pallas kernels for 15%

profile of v3, /device:TPU:1, one launch (start us, length us, event | category | flops | bytes accessed | tf_op | source)
XLA Modules:
  0.0 347.5 jit_solution(13900626513647481388)
XLA Ops:
  8.7 3.6 %collective-permute-start = (bf16[2,256,256]{2,1,0:T(8,128)(2,1)S(1)}, bf16[2,256,256]{2,1,0:T(8,128)(2,1)S(1)}, u32[]{:S(2)}, u32[]{:S(2)}) collective-permute-start(bf16[2,256,256]{2,1,0:T(8,128)(2,1)S(1)} %get-tuple-element.30), channel_id=1, source_target_pairs={{0,4},{4,0},{8,12},{12,8},{16,20},{20,16},{24,28},{28,24},{32,36},... | collective-permute-start | bytes 786440 | tf_op jit(solution)/shard_map/ppermute | solution.py:241
  12.4 5.6 %collective-permute-done = bf16[2,256,256]{2,1,0:T(8,128)(2,1)S(1)} collective-permute-done((bf16[2,256,256]{2,1,0:T(8,128)(2,1)S(1)}, bf16[2,256,256]{2,1,0:T(8,128)(2,1)S(1)}, u32[]{:S(2)}, u32[]{:S(2)}) %collective-permute-start) | collective-permute-done | bytes 262176 | tf_op jit(solution)/shard_map/ppermute | solution.py:241
  18.9 3.2 collective-permute-start.36
  22.1 4.9 %collective-permute-done.36 = bf16[2,256,256]{2,1,0:T(8,128)(2,1)S(1)} collective-permute-done((bf16[2,256,256]{2,1,0:T(8,128)(2,1)S(1)}, bf16[2,256,256]{2,1,0:T(8,128)(2,1)S(1)}, u32[]{:S(2)}, u32[]{:S(2)}) %collective-permute-start.36) | collective-permute-done | bytes 262176 | tf_op jit(solution)/shard_map/ppermute | solution.py:241
  27.9 3.0 collective-permute-start.4
  30.9 9.6 %collective-permute-done.4 = bf16[2,256,512]{2,1,0:T(8,128)(2,1)S(1)} collective-permute-done((bf16[2,256,512]{2,1,0:T(8,128)(2,1)S(1)}, bf16[2,256,512]{2,1,0:T(8,128)(2,1)S(1)}, u32[]{:S(2)}, u32[]{:S(2)}) %collective-permute-start.4) | collective-permute-done | bytes 524320 | tf_op jit(solution)/shard_map/ppermute | solution.py:241
  45.4 3.8 %collective-permute-start.5 = (bf16[2,256,512]{2,1,0:T(8,128)(2,1)S(1)}, bf16[2,256,512]{2,1,0:T(8,128)(2,1)S(1)}, u32[]{:S(2)}, u32[]{:S(2)}) collective-permute-start(bf16[2,256,512]{2,1,0:T(8,128)(2,1)S(1)} %get-tuple-element.32), channel_id=1, source_target_pairs={{0,24},{4,28},{8,0},{12,4},{16,8},{20,12},{24,16},{28,20},{32,56},... | collective-permute-start | bytes 1572872 | tf_op jit(solution)/shard_map/ppermute | solution.py:172
  49.2 8.3 %collective-permute-done.10 = bf16[2,256,512]{2,1,0:T(8,128)(2,1)S(1)} collective-permute-done((bf16[2,256,512]{2,1,0:T(8,128)(2,1)S(1)}, bf16[2,256,512]{2,1,0:T(8,128)(2,1)S(1)}, u32[]{:S(2)}, u32[]{:S(2)}) %collective-permute-start.10) | collective-permute-done | bytes 524320 | tf_op jit(solution)/shard_map/ppermute | solution.py:173
  57.5 18.1 %collective-permute-done.9 = bf16[2,256,512]{2,1,0:T(8,128)(2,1)S(1)} collective-permute-done((bf16[2,256,512]{2,1,0:T(8,128)(2,1)S(1)}, bf16[2,256,512]{2,1,0:T(8,128)(2,1)S(1)}, u32[]{:S(2)}, u32[]{:S(2)}) %collective-permute-start.9) | collective-permute-done | bytes 524320 | tf_op jit(solution)/shard_map/ppermute | solution.py:174
  75.8 11.2 %collective-permute-done.7 = bf16[2,256,512]{2,1,0:T(8,128)(2,1)S(1)} collective-permute-done((bf16[2,256,512]{2,1,0:T(8,128)(2,1)S(1)}, bf16[2,256,512]{2,1,0:T(8,128)(2,1)S(1)}, u32[]{:S(2)}, u32[]{:S(2)}) %collective-permute-start.7) | collective-permute-done | bytes 524320 | tf_op jit(solution)/shard_map/ppermute | solution.py:173
  92.1 30.8 %collective-permute-done.25.refs_1_ = bf16[8,256,256]{2,1,0:T(8,128)(2,1)S(1)} collective-permute-done((bf16[8,256,256]{2,1,0:T(8,128)(2,1)S(1)}, bf16[8,256,256]{2,1,0:T(8,128)(2,1)S(1)}, u32[]{:S(2)}, u32[]{:S(2)}) %collective-permute-start.25) | collective-permute-done | bytes 1048608 | tf_op jit(solution)/shard_map/ppermute | solution.py:184
  130.4 23.4 %collective-permute-done.11.refs_1_ = bf16[8,256,256]{2,1,0:T(8,128)(2,1)S(1)} collective-permute-done((bf16[8,256,256]{2,1,0:T(8,128)(2,1)S(1)}, bf16[8,256,256]{2,1,0:T(8,128)(2,1)S(1)}, u32[]{:S(2)}, u32[]{:S(2)}) %collective-permute-start.11) | collective-permute-done | bytes 1048608 | tf_op jit(solution)/shard_map/ppermute | solution.py:184
  158.8 4.8 %constant_dynamic-slice_fusion.2 = (bf16[1024,1024]{1,0:T(8,128)(2,1)}, bf16[1024,1024]{1,0:T(8,128)(2,1)}) fusion(bf16[1024,4096]{1,0:T(8,128)(2,1)} %param.10, s32[]{:T(128)S(6)} %select_n.291, s32[]{:T(128)S(6)} %select_n.290), kind=kLoop, calls=%fused_computation.46 | loop fusion | bytes 8388616 | tf_op jit(solution)/shard_map/dynamic_slice | solution.py:253
  165.8 8.8 %collective-permute-start.22 = (bf16[1024,1024]{1,0:T(8,128)(2,1)}, bf16[1024,1024]{1,0:T(8,128)(2,1)}, u32[]{:S(2)}, u32[]{:S(2)}) collective-permute-start(bf16[1024,1024]{1,0:T(8,128)(2,1)} %get-tuple-element.23), channel_id=1, source_target_pairs={{0,1},{1,0},{2,3},{3,2},{4,5},{5,4},{6,7},{7,6},{8,9},{9,8},{10,11... | collective-permute-start | bytes 6291464 | tf_op jit(solution)/shard_map/ppermute | solution.py:199
  176.6 6.3 %collective-permute-start.16 = (bf16[4,256,256]{2,1,0:T(8,128)(2,1)}, bf16[4,256,256]{2,1,0:T(8,128)(2,1)S(1)}, u32[]{:S(2)}, u32[]{:S(2)}) collective-permute-start(bf16[4,256,256]{2,1,0:T(8,128)(2,1)} %slice.88), channel_id=1, source_target_pairs={{0,24},{4,28},{8,0},{12,4},{16,8},{20,12},{24,16},{28,20},{32,56},... | collective-permute-start | bytes 1572872 | tf_op jit(solution)/shard_map/ppermute | solution.py:189
  182.9 4.3 %fusion.3 = (bf16[512,1024]{1,0:T(8,128)(2,1)}, bf16[512,1024]{1,0:T(8,128)(2,1)}, bf16[512,1024]{1,0:T(8,128)(2,1)}, bf16[512,1024]{1,0:T(8,128)(2,1)}) fusion(bf16[1024,4096]{1,0:T(8,128)(2,1)} %param.10, s32[]{:T(128)S(6)} %add.329, s32[]{:T(128)S(6)} %select_n.293, s32[]{:T(128)S(6)} %select_n.292), kind=kLoop, calls=%fused_computation.60 | loop fusion | bytes 8388620 | tf_op jit(solution)/shard_map/slice | solution.py:207
  189.2 12.2 %collective-permute-start.24 = (bf16[512,1024]{1,0:T(8,128)(2,1)}, bf16[512,1024]{1,0:T(8,128)(2,1)}, u32[]{:S(2)}, u32[]{:S(2)}) collective-permute-start(bf16[512,1024]{1,0:T(8,128)(2,1)} %get-tuple-element.20), channel_id=1, source_target_pairs={{0,3},{1,2},{2,1},{3,0},{4,7},{5,6},{6,5},{7,4},{8,11},{9,10},{10,... | collective-permute-start | bytes 3145736 | tf_op jit(solution)/shard_map/ppermute | solution.py:206
  204.9 3.3 collective-permute-start.38
  208.8 6.8 %attend.5.refs_4_ = bf16[1536,256]{1,0:T(8,128)(2,1)} custom-call(s32[4,24]{1,0:T(4,128)} %pad_add_fusion.1.spot_ref, bf16[1536,1024]{1,0:T(8,128)(2,1)} %q_hbm.7, bf16[8,256,256]{2,1,0:T(8,128)(2,1)} %copy-done.2, bf16[8,256,256]{2,1,0:T(8,128)(2,1)} %copy-done.9, bf16[4,256,256]{2,1,0:T(8,128)(2,1)} %collective-permute-done.12.refs_2_, ...), custom_call_target="tpu_custom_call" | custom-call | flops 402653184 | bytes 20971520 | tf_op jit(solution)/shard_map/attend/pallas_call | solution.py:113
  215.6 4.5 %collective-permute-done.32.refs_8_ = bf16[4,256,256]{2,1,0:T(8,128)(2,1)} collective-permute-done((bf16[4,256,256]{2,1,0:T(8,128)(2,1)}, bf16[4,256,256]{2,1,0:T(8,128)(2,1)}, u32[]{:S(2)}, u32[]{:S(2)}) %collective-permute-start.32) | collective-permute-done | bytes 524320 | tf_op jit(solution)/shard_map/ppermute | solution.py:190
  220.2 6.8 %attend.6.refs_0_ = bf16[1536,256]{1,0:T(8,128)(2,1)} custom-call(s32[4,24]{1,0:T(4,128)} %pad_add_fusion.1.spot_ref, bf16[1536,1024]{1,0:T(8,128)(2,1)} %q_hbm.7, bf16[8,256,256]{2,1,0:T(8,128)(2,1)} %copy-done, bf16[8,256,256]{2,1,0:T(8,128)(2,1)} %copy-done.5, bf16[4,256,256]{2,1,0:T(8,128)(2,1)} %collective-permute-done.26.refs_2_, ...), custom_call_target="tpu_custom_call" | custom-call | flops 402653184 | bytes 20971520 | tf_op jit(solution)/shard_map/attend/pallas_call | solution.py:113
  229.1 6.9 %attend.4.refs_0_ = bf16[1536,256]{1,0:T(8,128)(2,1)} custom-call(s32[4,24]{1,0:T(4,128)} %pad_add_fusion.spot_ref, bf16[1536,1024]{1,0:T(8,128)(2,1)} %q_hbm.7, bf16[64,256,256]{2,1,0:T(8,128)(2,1)} %all-gather.3.cloned.1.call-done.refs_0_.refs_1_, bf16[64,256,256]{2,1,0:T(8,128)(2,1)} %all-gather.3.cloned.1.call-done.refs_0_.refs_1_), custom_call_target="tpu_custom_call" | custom-call | flops 402653184 | bytes 20971520 | tf_op jit(solution)/shard_map/attend/pallas_call | solution.py:113
  236.0 7.0 %collective-permute-done.24.refs_11_.refs_15_ = bf16[512,1024]{1,0:T(8,128)(2,1)} collective-permute-done((bf16[512,1024]{1,0:T(8,128)(2,1)}, bf16[512,1024]{1,0:T(8,128)(2,1)}, u32[]{:S(2)}, u32[]{:S(2)}) %collective-permute-start.24) | collective-permute-done | bytes 1048608 | tf_op jit(solution)/shard_map/ppermute | solution.py:206
  244.5 6.8 %attend.7.refs_4_ = bf16[1536,256]{1,0:T(8,128)(2,1)} custom-call(s32[4,24]{1,0:T(4,128)} %pad_add_fusion.spot_ref, bf16[1536,1024]{1,0:T(8,128)(2,1)} %q_hbm.7, bf16[64,256,256]{2,1,0:T(8,128)(2,1)} %all-gather.5.cloned.1.call-done.refs_0_.refs_1_, bf16[64,256,256]{2,1,0:T(8,128)(2,1)} %all-gather.5.cloned.1.call-done.refs_0_.refs_1_), custom_call_target="tpu_custom_call" | custom-call | flops 402653184 | bytes 20971520 | tf_op jit(solution)/shard_map/attend/pallas_call | solution.py:113
  251.3 9.3 %collective-permute-start.21 = (bf16[1536,256]{1,0:T(8,128)(2,1)}, bf16[1536,256]{1,0:T(8,128)(2,1)}, u32[]{:S(2)}, u32[]{:S(2)}) collective-permute-start(bf16[1536,256]{1,0:T(8,128)(2,1)} %collective-permute-done.20.refs_6_), channel_id=1, source_target_pairs={{0,1},{1,0},{2,3},{3,2},{4,5},{5,4},{6,7},{7,6},{8,9},{9,8},{10,11... | collective-permute-start | bytes 2359304 | tf_op jit(solution)/shard_map/ppermute | solution.py:265
  263.3 16.4 %collective-permute-done.2.refs_2_ = bf16[1536,256]{1,0:T(8,128)(2,1)} collective-permute-done((bf16[1536,256]{1,0:T(8,128)(2,1)}, bf16[1536,256]{1,0:T(8,128)(2,1)}, u32[]{:S(2)}, u32[]{:S(2)}) %collective-permute-start.2) | collective-permute-done | bytes 786464 | tf_op jit(solution)/shard_map/ppermute | solution.py:264
  279.7 14.5 %collective-permute-start.3 = (bf16[1536,256]{1,0:T(8,128)(2,1)}, bf16[1536,256]{1,0:T(8,128)(2,1)}, u32[]{:S(2)}, u32[]{:S(2)}) collective-permute-start(bf16[1536,256]{1,0:T(8,128)(2,1)} %collective-permute-done.2.refs_2_), channel_id=1, source_target_pairs={{0,1},{1,0},{2,3},{3,2},{4,5},{5,4},{6,7},{7,6},{8,9},{9,8},{10,11... | collective-permute-start | bytes 2359304 | tf_op jit(solution)/shard_map/ppermute | solution.py:265
  297.3 6.7 %collective-permute-start.37 = (bf16[1536,256]{1,0:T(8,128)(2,1)}, bf16[1536,256]{1,0:T(8,128)(2,1)}, u32[]{:S(2)}, u32[]{:S(2)}) collective-permute-start(bf16[1536,256]{1,0:T(8,128)(2,1)} %attend.7.refs_4_), channel_id=1, source_target_pairs={{0,1},{1,0},{2,3},{3,2},{4,5},{5,4},{6,7},{7,6},{8,9},{9,8},{10,11... | collective-permute-start | bytes 2359304 | tf_op jit(solution)/shard_map/ppermute | solution.py:263
  304.1 12.6 %shard_map.64.base_ref = f32[1536,1024]{1,0:T(8,128)} custom-call(bf16[1536,1024]{1,0:T(8,128)(2,1)} %base_ref.1, bf16[1536,256]{1,0:T(8,128)(2,1)} %attend.4.refs_0_, bf16[1536,256]{1,0:T(8,128)(2,1)} %collective-permute-done.1.refs_1_, bf16[1536,256]{1,0:T(8,128)(2,1)} %collective-permute-done.2.refs_2_, bf16[1536,256]{1,0:T(8,128)(2,1)} %collective-permute-done.3.refs_3_, ...), custom_call_target="tpu_custom_call" | custom-call | flops 6442450944 | bytes 20971520 | tf_op jit(solution)/shard_map/pallas_call | solution.py:156
  316.7 3.9 %collective-permute-done.39.refs_9_.refs_3_ = bf16[512,1024]{1,0:T(8,128)(2,1)} collective-permute-done((bf16[512,1024]{1,0:T(8,128)(2,1)}, bf16[512,1024]{1,0:T(8,128)(2,1)}, u32[]{:S(2)}, u32[]{:S(2)}) %collective-permute-start.39) | collective-permute-done | bytes 1048608 | tf_op jit(solution)/shard_map/ppermute | solution.py:207
  320.6 11.5 %shard_map.65.base_ref = f32[1536,1024]{1,0:T(8,128)} custom-call(f32[1536,1024]{1,0:T(8,128)} %shard_map.64.base_ref, bf16[1536,256]{1,0:T(8,128)(2,1)} %attend.6.refs_0_, bf16[1536,256]{1,0:T(8,128)(2,1)} %collective-permute-done.33.refs_1_, bf16[1536,256]{1,0:T(8,128)(2,1)} %collective-permute-done.34.refs_2_, ...), custom_call_target="tpu_custom_call" | custom-call | flops 4831838208 | bytes 20971520 | tf_op jit(solution)/shard_map/pallas_call | solution.py:156
  333.0 7.6 %shard_map.66 = bf16[1536,1024]{1,0:T(8,128)(2,1)} custom-call(f32[1536,1024]{1,0:T(8,128)} %shard_map.65.base_ref, bf16[1536,256]{1,0:T(8,128)(2,1)} %collective-permute-done.40.refs_0_, bf16[1536,256]{1,0:T(8,128)(2,1)} %copy-done.13, bf16[512,1024]{1,0:T(8,128)(2,1)} %collective-permute-done.38.refs_8_.refs_2_, ...), custom_call_target="tpu_custom_call" | custom-call | flops 1610612736 | bytes 20971520 | tf_op jit(solution)/shard_map/pallas_call | solution.py:156
  (125 shorter events, 47.3 us)
Async XLA Ops:
  6.5 222.6 %all-gather.3.cloned.1.call-start = ((), (), s32[]{:S(2)}) async-start(), calls=%async_computation | async-start | bytes 8912896 | tf_op jit(solution)/shard_map/all_gather | solution.py:195
  18.9 225.6 %all-gather.5.cloned.1.call-start = ((), (), s32[]{:S(2)}) async-start(), calls=%async_computation.1 | async-start | bytes 8912896 | tf_op jit(solution)/shard_map/all_gather | solution.py:195
  43.8 31.7 %collective-permute-start.9 = (bf16[2,256,512]{2,1,0:T(8,128)(2,1)S(1)}, bf16[2,256,512]{2,1,0:T(8,128)(2,1)S(1)}, u32[]{:S(2)}, u32[]{:S(2)}) collective-permute-start(bf16[2,256,512]{2,1,0:T(8,128)(2,1)S(1)} %get-tuple-element.31), channel_id=1, source_target_pairs={{0,64},{4,68},{8,72},{12,76},{16,80},{20,84},{24,88},{28,92},{32,9... | collective-permute-start | bytes 1572872 | tf_op jit(solution)/shard_map/ppermute | solution.py:174
  45.4 30.4 %collective-permute-start.5 = (bf16[2,256,512]{2,1,0:T(8,128)(2,1)S(1)}, bf16[2,256,512]{2,1,0:T(8,128)(2,1)S(1)}, u32[]{:S(2)}, u32[]{:S(2)}) collective-permute-start(bf16[2,256,512]{2,1,0:T(8,128)(2,1)S(1)} %get-tuple-element.32), channel_id=1, source_target_pairs={{0,24},{4,28},{8,0},{12,4},{16,8},{20,12},{24,16},{28,20},{32,56},... | collective-permute-start | bytes 1572872 | tf_op jit(solution)/shard_map/ppermute | solution.py:172
  49.2 26.7 %collective-permute-start.6 = (bf16[2,256,512]{2,1,0:T(8,128)(2,1)S(1)}, bf16[2,256,512]{2,1,0:T(8,128)(2,1)S(1)}, u32[]{:S(2)}, u32[]{:S(2)}) collective-permute-start(bf16[2,256,512]{2,1,0:T(8,128)(2,1)S(1)} %get-tuple-element.32), channel_id=1, source_target_pairs={{0,16},{4,20},{8,24},{12,28},{16,0},{20,4},{24,8},{28,12},{32,48},... | collective-permute-start | bytes 1572872 | tf_op jit(solution)/shard_map/ppermute | solution.py:174
  57.5 29.6 %collective-permute-start.7 = (bf16[2,256,512]{2,1,0:T(8,128)(2,1)S(1)}, bf16[2,256,512]{2,1,0:T(8,128)(2,1)S(1)}, u32[]{:S(2)}, u32[]{:S(2)}) collective-permute-start(bf16[2,256,512]{2,1,0:T(8,128)(2,1)S(1)} %get-tuple-element.32), channel_id=1, source_target_pairs={{0,8},{4,12},{8,16},{12,20},{16,24},{20,28},{24,0},{28,4},{32,40},... | collective-permute-start | bytes 1572872 | tf_op jit(solution)/shard_map/ppermute | solution.py:173
  87.6 35.3 %collective-permute-start.25 = (bf16[8,256,256]{2,1,0:T(8,128)(2,1)S(1)}, bf16[8,256,256]{2,1,0:T(8,128)(2,1)S(1)}, u32[]{:S(2)}, u32[]{:S(2)}) collective-permute-start(bf16[8,256,256]{2,1,0:T(8,128)(2,1)S(1)} %get-tuple-element.27.refs_0_), channel_id=1, source_target_pairs={{0,96},{4,100},{8,104},{12,108},{16,112},{20,116},{24,120},{28,124... | collective-permute-start | bytes 3145736 | tf_op jit(solution)/shard_map/ppermute | solution.py:184
  87.6 36.0 %collective-permute-start.27 = (bf16[8,256,256]{2,1,0:T(8,128)(2,1)S(1)}, bf16[8,256,256]{2,1,0:T(8,128)(2,1)S(1)}, u32[]{:S(2)}, u32[]{:S(2)}) collective-permute-start(bf16[8,256,256]{2,1,0:T(8,128)(2,1)S(1)} %get-tuple-element.27.refs_0_), channel_id=1, source_target_pairs={{0,32},{4,36},{8,40},{12,44},{16,48},{20,52},{24,56},{28,60},{32,6... | collective-permute-start | bytes 3145736 | tf_op jit(solution)/shard_map/ppermute | solution.py:184
  89.3 35.2 %collective-permute-start.29 = (bf16[8,256,256]{2,1,0:T(8,128)(2,1)S(1)}, bf16[8,256,256]{2,1,0:T(8,128)(2,1)S(1)}, u32[]{:S(2)}, u32[]{:S(2)}) collective-permute-start(bf16[8,256,256]{2,1,0:T(8,128)(2,1)S(1)} %get-tuple-element.25.refs_5_), channel_id=1, source_target_pairs={{0,24},{4,28},{8,0},{12,4},{16,8},{20,12},{24,16},{28,20},{32,56},... | collective-permute-start | bytes 3145736 | tf_op jit(solution)/shard_map/ppermute | solution.py:184
  89.3 38.5 %collective-permute-start.31 = (bf16[8,256,256]{2,1,0:T(8,128)(2,1)S(1)}, bf16[8,256,256]{2,1,0:T(8,128)(2,1)S(1)}, u32[]{:S(2)}, u32[]{:S(2)}) collective-permute-start(bf16[8,256,256]{2,1,0:T(8,128)(2,1)S(1)} %get-tuple-element.25.refs_5_), channel_id=1, source_target_pairs={{0,8},{4,12},{8,16},{12,20},{16,24},{20,28},{24,0},{28,4},{32,40},... | collective-permute-start | bytes 3145736 | tf_op jit(solution)/shard_map/ppermute | solution.py:184
  90.8 62.9 %collective-permute-start.11 = (bf16[8,256,256]{2,1,0:T(8,128)(2,1)S(1)}, bf16[8,256,256]{2,1,0:T(8,128)(2,1)S(1)}, u32[]{:S(2)}, u32[]{:S(2)}) collective-permute-start(bf16[8,256,256]{2,1,0:T(8,128)(2,1)S(1)} %get-tuple-element.28.refs_0_), channel_id=1, source_target_pairs={{0,96},{4,100},{8,104},{12,108},{16,112},{20,116},{24,120},{28,124... | collective-permute-start | bytes 3145736 | tf_op jit(solution)/shard_map/ppermute | solution.py:184
  122.9 31.2 %collective-permute-start.13 = (bf16[8,256,256]{2,1,0:T(8,128)(2,1)S(1)}, bf16[8,256,256]{2,1,0:T(8,128)(2,1)S(1)}, u32[]{:S(2)}, u32[]{:S(2)}) collective-permute-start(bf16[8,256,256]{2,1,0:T(8,128)(2,1)S(1)} %get-tuple-element.28.refs_0_), channel_id=1, source_target_pairs={{0,32},{4,36},{8,40},{12,44},{16,48},{20,52},{24,56},{28,60},{32,6... | collective-permute-start | bytes 3145736 | tf_op jit(solution)/shard_map/ppermute | solution.py:184
  123.7 31.4 %collective-permute-start.15 = (bf16[8,256,256]{2,1,0:T(8,128)(2,1)S(1)}, bf16[8,256,256]{2,1,0:T(8,128)(2,1)S(1)}, u32[]{:S(2)}, u32[]{:S(2)}) collective-permute-start(bf16[8,256,256]{2,1,0:T(8,128)(2,1)S(1)} %get-tuple-element.26.refs_5_), channel_id=1, source_target_pairs={{0,24},{4,28},{8,0},{12,4},{16,8},{20,12},{24,16},{28,20},{32,56},... | collective-permute-start | bytes 3145736 | tf_op jit(solution)/shard_map/ppermute | solution.py:184
  124.4 34.3 %collective-permute-start.17 = (bf16[8,256,256]{2,1,0:T(8,128)(2,1)S(1)}, bf16[8,256,256]{2,1,0:T(8,128)(2,1)}, u32[]{:S(2)}, u32[]{:S(2)}) collective-permute-start(bf16[8,256,256]{2,1,0:T(8,128)(2,1)S(1)} %get-tuple-element.26.refs_5_), channel_id=1, source_target_pairs={{0,8},{4,12},{8,16},{12,20},{16,24},{20,28},{24,0},{28,4},{32,40},... | collective-permute-start | bytes 3145736 | tf_op jit(solution)/shard_map/ppermute | solution.py:184
  127.8 38.0 %collective-permute-start.26 = (bf16[4,256,256]{2,1,0:T(8,128)(2,1)}, bf16[4,256,256]{2,1,0:T(8,128)(2,1)}, u32[]{:S(2)}, u32[]{:S(2)}) collective-permute-start(bf16[4,256,256]{2,1,0:T(8,128)(2,1)} %slice.90), channel_id=1, source_target_pairs={{0,96},{4,100},{8,104},{12,108},{16,112},{20,116},{24,120},{28,124... | collective-permute-start | bytes 1572872 | tf_op jit(solution)/shard_map/ppermute | solution.py:189
  154.1 28.7 %collective-permute-start.30 = (bf16[4,256,256]{2,1,0:T(8,128)(2,1)}, bf16[4,256,256]{2,1,0:T(8,128)(2,1)}, u32[]{:S(2)}, u32[]{:S(2)}) collective-permute-start(bf16[4,256,256]{2,1,0:T(8,128)(2,1)} %slice.92), channel_id=1, source_target_pairs={{0,24},{4,28},{8,0},{12,4},{16,8},{20,12},{24,16},{28,20},{32,56},... | collective-permute-start | bytes 1572872 | tf_op jit(solution)/shard_map/ppermute | solution.py:189
  155.1 33.2 %collective-permute-start.12 = (bf16[4,256,256]{2,1,0:T(8,128)(2,1)}, bf16[4,256,256]{2,1,0:T(8,128)(2,1)}, u32[]{:S(2)}, u32[]{:S(2)}) collective-permute-start(bf16[4,256,256]{2,1,0:T(8,128)(2,1)} %slice.86), channel_id=1, source_target_pairs={{0,96},{4,100},{8,104},{12,108},{16,112},{20,116},{24,120},{28,124... | collective-permute-start | bytes 1572872 | tf_op jit(solution)/shard_map/ppermute | solution.py:189
  158.8 30.5 %collective-permute-start.14 = (bf16[4,256,256]{2,1,0:T(8,128)(2,1)}, bf16[4,256,256]{2,1,0:T(8,128)(2,1)}, u32[]{:S(2)}, u32[]{:S(2)}) collective-permute-start(bf16[4,256,256]{2,1,0:T(8,128)(2,1)} %slice.87), channel_id=1, source_target_pairs={{0,32},{4,36},{8,40},{12,44},{16,48},{20,52},{24,56},{28,60},{32,6... | collective-permute-start | bytes 1572872 | tf_op jit(solution)/shard_map/ppermute | solution.py:190
  165.8 94.8 %collective-permute-start.22 = (bf16[1024,1024]{1,0:T(8,128)(2,1)}, bf16[1024,1024]{1,0:T(8,128)(2,1)}, u32[]{:S(2)}, u32[]{:S(2)}) collective-permute-start(bf16[1024,1024]{1,0:T(8,128)(2,1)} %get-tuple-element.23), channel_id=1, source_target_pairs={{0,1},{1,0},{2,3},{3,2},{4,5},{5,4},{6,7},{7,6},{8,9},{9,8},{10,11... | collective-permute-start | bytes 6291464 | tf_op jit(solution)/shard_map/ppermute | solution.py:199
  176.6 28.3 %collective-permute-start.16 = (bf16[4,256,256]{2,1,0:T(8,128)(2,1)}, bf16[4,256,256]{2,1,0:T(8,128)(2,1)S(1)}, u32[]{:S(2)}, u32[]{:S(2)}) collective-permute-start(bf16[4,256,256]{2,1,0:T(8,128)(2,1)} %slice.88), channel_id=1, source_target_pairs={{0,24},{4,28},{8,0},{12,4},{16,8},{20,12},{24,16},{28,20},{32,56},... | collective-permute-start | bytes 1572872 | tf_op jit(solution)/shard_map/ppermute | solution.py:189
  188.3 38.7 %collective-permute-start.23 = (bf16[512,1024]{1,0:T(8,128)(2,1)}, bf16[512,1024]{1,0:T(8,128)(2,1)}, u32[]{:S(2)}, u32[]{:S(2)}) collective-permute-start(bf16[512,1024]{1,0:T(8,128)(2,1)} %get-tuple-element.21), channel_id=1, source_target_pairs={{0,2},{1,3},{2,0},{3,1},{4,6},{5,7},{6,4},{7,5},{8,10},{9,11},{10,... | collective-permute-start | bytes 3145736 | tf_op jit(solution)/shard_map/ppermute | solution.py:202
  189.2 53.8 %collective-permute-start.24 = (bf16[512,1024]{1,0:T(8,128)(2,1)}, bf16[512,1024]{1,0:T(8,128)(2,1)}, u32[]{:S(2)}, u32[]{:S(2)}) collective-permute-start(bf16[512,1024]{1,0:T(8,128)(2,1)} %get-tuple-element.20), channel_id=1, source_target_pairs={{0,3},{1,2},{2,1},{3,0},{4,7},{5,6},{6,5},{7,4},{8,11},{9,10},{10,... | collective-permute-start | bytes 3145736 | tf_op jit(solution)/shard_map/ppermute | solution.py:206
  204.9 39.6 %collective-permute-start.38 = (bf16[512,1024]{1,0:T(8,128)(2,1)}, bf16[512,1024]{1,0:T(8,128)(2,1)}, u32[]{:S(2)}, u32[]{:S(2)}) collective-permute-start(bf16[512,1024]{1,0:T(8,128)(2,1)} %get-tuple-element.22), channel_id=1, source_target_pairs={{0,6},{1,7},{2,4},{3,5},{4,2},{5,3},{6,0},{7,1},{8,14},{9,15},{10,... | collective-permute-start | bytes 3145736 | tf_op jit(solution)/shard_map/ppermute | solution.py:203
  220.2 31.1 %collective-permute-start.20 = (bf16[1536,256]{1,0:T(8,128)(2,1)}, bf16[1536,256]{1,0:T(8,128)(2,1)}, u32[]{:S(2)}, u32[]{:S(2)}) collective-permute-start(bf16[1536,256]{1,0:T(8,128)(2,1)} %attend.5.refs_4_), channel_id=1, source_target_pairs={{0,2},{1,3},{2,0},{3,1},{4,6},{5,7},{6,4},{7,5},{8,10},{9,11},{10,... | collective-permute-start | bytes 2359304 | tf_op jit(solution)/shard_map/ppermute | solution.py:264
  227.0 35.9 %collective-permute-start.34 = (bf16[1536,256]{1,0:T(8,128)(2,1)}, bf16[1536,256]{1,0:T(8,128)(2,1)}, u32[]{:S(2)}, u32[]{:S(2)}) collective-permute-start(bf16[1536,256]{1,0:T(8,128)(2,1)} %attend.6.refs_0_), channel_id=1, source_target_pairs={{0,2},{1,3},{2,0},{3,1},{4,6},{5,7},{6,4},{7,5},{8,10},{9,11},{10,... | collective-permute-start | bytes 2359304 | tf_op jit(solution)/shard_map/ppermute | solution.py:264
  243.0 36.7 %collective-permute-start.2 = (bf16[1536,256]{1,0:T(8,128)(2,1)}, bf16[1536,256]{1,0:T(8,128)(2,1)}, u32[]{:S(2)}, u32[]{:S(2)}) collective-permute-start(bf16[1536,256]{1,0:T(8,128)(2,1)} %attend.4.refs_0_), channel_id=1, source_target_pairs={{0,2},{1,3},{2,0},{3,1},{4,6},{5,7},{6,4},{7,5},{8,10},{9,11},{10,... | collective-permute-start | bytes 2359304 | tf_op jit(solution)/shard_map/ppermute | solution.py:264
  244.5 49.8 %collective-permute-start.19 = (bf16[1536,256]{1,0:T(8,128)(2,1)S(1)}, bf16[1536,256]{1,0:T(8,128)(2,1)}, u32[]{:S(2)}, u32[]{:S(2)}) collective-permute-start(bf16[1536,256]{1,0:T(8,128)(2,1)S(1)} %copy-done.4), channel_id=1, source_target_pairs={{0,1},{1,0},{2,3},{3,2},{4,5},{5,4},{6,7},{7,6},{8,9},{9,8},{10,11... | collective-permute-start | bytes 2359304 | tf_op jit(solution)/shard_map/ppermute | solution.py:263
  251.3 45.4 %collective-permute-start.21 = (bf16[1536,256]{1,0:T(8,128)(2,1)}, bf16[1536,256]{1,0:T(8,128)(2,1)}, u32[]{:S(2)}, u32[]{:S(2)}) collective-permute-start(bf16[1536,256]{1,0:T(8,128)(2,1)} %collective-permute-done.20.refs_6_), channel_id=1, source_target_pairs={{0,1},{1,0},{2,3},{3,2},{4,5},{5,4},{6,7},{7,6},{8,9},{9,8},{10,11... | collective-permute-start | bytes 2359304 | tf_op jit(solution)/shard_map/ppermute | solution.py:265
  260.6 36.7 %collective-permute-start.1 = (bf16[1536,256]{1,0:T(8,128)(2,1)}, bf16[1536,256]{1,0:T(8,128)(2,1)}, u32[]{:S(2)}, u32[]{:S(2)}) collective-permute-start(bf16[1536,256]{1,0:T(8,128)(2,1)} %attend.4.refs_0_), channel_id=1, source_target_pairs={{0,1},{1,0},{2,3},{3,2},{4,5},{5,4},{6,7},{7,6},{8,9},{9,8},{10,11... | collective-permute-start | bytes 2359304 | tf_op jit(solution)/shard_map/ppermute | solution.py:263
  262.9 34.5 %collective-permute-start.40 = (bf16[1536,256]{1,0:T(8,128)(2,1)}, bf16[1536,256]{1,0:T(8,128)(2,1)}, u32[]{:S(2)}, u32[]{:S(2)}) collective-permute-start(bf16[1536,256]{1,0:T(8,128)(2,1)} %attend.7.refs_4_), channel_id=1, source_target_pairs={{0,2},{1,3},{2,0},{3,1},{4,6},{5,7},{6,4},{7,5},{8,10},{9,11},{10,... | collective-permute-start | bytes 2359304 | tf_op jit(solution)/shard_map/ppermute | solution.py:264
  294.3 26.3 %collective-permute-start.39 = (bf16[512,1024]{1,0:T(8,128)(2,1)}, bf16[512,1024]{1,0:T(8,128)(2,1)}, u32[]{:S(2)}, u32[]{:S(2)}) collective-permute-start(bf16[512,1024]{1,0:T(8,128)(2,1)} %get-tuple-element.19), channel_id=1, source_target_pairs={{0,7},{1,6},{2,5},{3,4},{4,3},{5,2},{6,1},{7,0},{8,15},{9,14},{10,... | collective-permute-start | bytes 3145736 | tf_op jit(solution)/shard_map/ppermute | solution.py:207
  304.1 28.1 %collective-permute-start.41 = (bf16[1536,256]{1,0:T(8,128)(2,1)}, bf16[1536,256]{1,0:T(8,128)(2,1)S(1)}, u32[]{:S(2)}, u32[]{:S(2)}) collective-permute-start(bf16[1536,256]{1,0:T(8,128)(2,1)} %collective-permute-done.40.refs_0_), channel_id=1, source_target_pairs={{0,1},{1,0},{2,3},{3,2},{4,5},{5,4},{6,7},{7,6},{8,9},{9,8},{10,11... | collective-permute-start | bytes 2359304 | tf_op jit(solution)/shard_map/ppermute | solution.py:265
  (28 other events, 630.6 us)
Sparse Core Ops, SparseCore 0:
  19.0 102.6 all-gather.2
  123.8 91.5 all-gather.4
